TPU v7x, 32 devices: a whole 2x2x4 slice. The times are simulated.
32 devices in a mesh: tm: 4 (over y, core), space: 8 (over z, x).
Axes of the slice: x: 2, y: 2, z: 4, core: 2. Of those that a mesh axis runs over, the one named last changes fastest.
Arguments:
- observed: float32 [8, 48, 1440], P('tm', 'space'), may hold values from -8 to 8
- noise_var: float32 [8], replicated, may hold values from 0.05 to 1
- spectral_var: float32 [1440, 48], P('space'), may hold values from 0.2 to 5
- time_scale: float32 [1440, 48], P('space'), may hold values from 1.5 to 2
Outputs:
- smoothed: float32 [8, 48, 1440], P('tm', 'space')
All inputs are finite; a program needn't handle non-finite values.
Results may differ from a plain program's by a relative error of at most 0.00007.
Values sent between devices are 32-bit elements; how exact they have to be, the bound alone decides.
A program may use at most 64 MiB of HBM per device.

v0:
```python
import functools
import math

import jax
import jax.numpy as jnp
import numpy as np
from jax import lax
from jax.experimental import pallas as pl
from jax.experimental.pallas import tpu as pltpu
from jax.sharding import PartitionSpec as P

HIGHEST = lax.Precision.HIGHEST
ROOT_FIVE = 2.23606797749979
NILPOTENT = ((1.0, 1.0, 0.0), (0.0, 1.0, 1.0), (-1.0, -3.0, -2.0))
NILPOTENT_SQUARED = ((1.0, 2.0, 1.0), (-1.0, -2.0, -1.0), (1.0, 2.0, 1.0))
STATIONARY = ((1.0, 0.0, -1.0 / 3.0), (0.0, 1.0 / 3.0, 0.0), (-1.0 / 3.0, 0.0, 1.0))


def lon_basis(size):
    mode_index = lax.broadcasted_iota(jnp.int32, (size, size), 0)
    longitude = lax.broadcasted_iota(jnp.int32, (size, size), 1)
    half_size = size // 2
    sine_rows = mode_index > half_size
    frequency = jnp.where(sine_rows, mode_index - half_size, mode_index)
    radians = (frequency * longitude % size).astype(jnp.float32) * (2.0 * math.pi / size)
    waveform = jnp.where(sine_rows, jnp.sin(radians), jnp.cos(radians))
    edge_rows = (mode_index == 0) | (mode_index == half_size)
    weight = jnp.where(edge_rows, math.sqrt(1.0 / size), math.sqrt(2.0 / size))
    return waveform * weight


def lat_basis(size):
    wavenumber = lax.broadcasted_iota(jnp.int32, (size, size), 0)
    latitude = lax.broadcasted_iota(jnp.int32, (size, size), 1)
    radians = (wavenumber * (2 * latitude + 1) % (4 * size)).astype(jnp.float32) * (
        math.pi / (2.0 * size)
    )
    weight = jnp.where(wavenumber == 0, math.sqrt(1.0 / size), math.sqrt(2.0 / size))
    return jnp.cos(radians) * weight


def mat_mul(left, right):
    return [
        [
            left[across][0] * right[0][within]
            + left[across][1] * right[1][within]
            + left[across][2] * right[2][within]
            for within in range(3)
        ]
        for across in range(3)
    ]


def mat_vec(matrix, vector):
    return [
        matrix[across][0] * vector[0]
        + matrix[across][1] * vector[1]
        + matrix[across][2] * vector[2]
        for across in range(3)
    ]


def transposed(matrix):
    return [[matrix[within][across] for within in range(3)] for across in range(3)]


def inverted(matrix):
    cofactor = [
        [
            matrix[1][1] * matrix[2][2] - matrix[1][2] * matrix[2][1],
            matrix[0][2] * matrix[2][1] - matrix[0][1] * matrix[2][2],
            matrix[0][1] * matrix[1][2] - matrix[0][2] * matrix[1][1],
        ],
        [
            matrix[1][2] * matrix[2][0] - matrix[1][0] * matrix[2][2],
            matrix[0][0] * matrix[2][2] - matrix[0][2] * matrix[2][0],
            matrix[0][2] * matrix[1][0] - matrix[0][0] * matrix[1][2],
        ],
        [
            matrix[1][0] * matrix[2][1] - matrix[1][1] * matrix[2][0],
            matrix[0][1] * matrix[2][0] - matrix[0][0] * matrix[2][1],
            matrix[0][0] * matrix[1][1] - matrix[0][1] * matrix[1][0],
        ],
    ]
    determinant = (
        matrix[0][0] * cofactor[0][0]
        + matrix[0][1] * cofactor[1][0]
        + matrix[0][2] * cofactor[2][0]
    )
    return [[cofactor[across][within] / determinant for within in range(3)] for across in range(3)]


def model_terms(variance, scale):
    decay_rate = ROOT_FIVE / scale
    damping = jnp.exp(-decay_rate)
    transition = [
        [
            damping
            * (
                (1.0 if across == within else 0.0)
                + decay_rate * NILPOTENT[across][within]
                + 0.5 * decay_rate * decay_rate * NILPOTENT_SQUARED[across][within]
            )
            for within in range(3)
        ]
        for across in range(3)
    ]
    stationary = [
        [variance * STATIONARY[across][within] for within in range(3)] for across in range(3)
    ]
    carried = mat_mul(mat_mul(transition, stationary), transposed(transition))
    process_noise = [
        [stationary[across][within] - carried[across][within] for within in range(3)]
        for across in range(3)
    ]
    return (transition, stationary, process_noise)


def predict_cov(covariance, transition, process_noise):
    carried = mat_mul(mat_mul(transition, covariance), transposed(transition))
    return [
        [carried[across][within] + process_noise[across][within] for within in range(3)]
        for across in range(3)
    ]


def gain_and_cov(predicted_cov, noise):
    innovation_var = predicted_cov[0][0] + noise
    kalman_gain = [predicted_cov[across][0] / innovation_var for across in range(3)]
    covariance = [
        [
            predicted_cov[across][within] - kalman_gain[across] * predicted_cov[0][within]
            for within in range(3)
        ]
        for across in range(3)
    ]
    return (kalman_gain, covariance)


def smooth_series(spectra, noise_var, variance, scale):
    transition, stationary, process_noise = model_terms(variance, scale)
    zeros = jnp.zeros_like(variance)

    def forward(carry, inputs):
        mean_state, covariance = carry
        observed, noise = inputs
        predicted_cov = predict_cov(covariance, transition, process_noise)
        smoother_gain = mat_mul(
            mat_mul(covariance, transposed(transition)), inverted(predicted_cov)
        )
        predicted = mat_vec(transition, mean_state)
        kalman_gain, covariance = gain_and_cov(predicted_cov, noise)
        residual = observed - predicted[0]
        mean_state = [predicted[across] + kalman_gain[across] * residual for across in range(3)]
        return ((mean_state, covariance), (mean_state, smoother_gain))

    _, (means, gains) = lax.scan(forward, ([zeros, zeros, zeros], stationary), (spectra, noise_var))

    def backward(later, inputs):
        mean_state, smoother_gain = inputs
        projected = mat_vec(transition, mean_state)
        difference = [later[across] - projected[across] for across in range(3)]
        correction = mat_vec(smoother_gain, difference)
        smoothed_state = [mean_state[across] + correction[across] for across in range(3)]
        return (smoothed_state, smoothed_state[0])

    last_state = [means[across][-1] for across in range(3)]
    earlier_means = [means[across][:-1] for across in range(3)]
    next_gains = [[gains[across][within][1:] for within in range(3)] for across in range(3)]
    _, field = lax.scan(backward, last_state, (earlier_means, next_gains), reverse=True)
    return jnp.concatenate([field, last_state[0][None]], axis=0)


def per_device_general(observed, noise_var, spectral_var, time_scale):
    hours_dev, lat_dev, lon_size = observed.shape
    band_count = lax.axis_size("space")
    lat_size = lat_dev * band_count
    modes_dev = lon_size // band_count
    lon_table = lon_basis(lon_size)
    lat_table = lat_basis(lat_size).reshape(lat_size, band_count, lat_dev)
    grid_rows = observed.reshape(hours_dev * lat_dev, lon_size)
    spectra = lax.dot_general(lon_table, grid_rows, (((1,), (1,)), ((), ())), precision=HIGHEST)
    by_mode = lax.all_to_all(spectra, "space", split_axis=0, concat_axis=1, tiled=True)
    by_mode = by_mode.reshape(modes_dev, band_count, hours_dev, lat_dev)
    coefficients = jnp.einsum("msha,nsa->hmn", by_mode, lat_table, precision=HIGHEST)
    flat = coefficients.reshape(hours_dev, modes_dev * lat_size)
    hourly = lax.all_to_all(flat, "tm", split_axis=1, concat_axis=0, tiled=True)
    share = flat.shape[1] // lax.axis_size("tm")
    offset = lax.axis_index("tm") * share
    variance = lax.dynamic_slice_in_dim(spectral_var.reshape(-1), offset, share)
    scale = lax.dynamic_slice_in_dim(time_scale.reshape(-1), offset, share)
    series = smooth_series(hourly, noise_var, variance, scale)
    smooth = lax.all_to_all(series, "tm", split_axis=0, concat_axis=1, tiled=True).reshape(
        hours_dev, modes_dev, lat_size
    )
    latitude_grid = jnp.einsum("hmn,nsa->msha", smooth, lat_table, precision=HIGHEST)
    latitude_grid = latitude_grid.reshape(modes_dev, band_count * hours_dev * lat_dev)
    by_band = lax.all_to_all(latitude_grid, "space", split_axis=1, concat_axis=0, tiled=True)
    field = lax.dot_general(by_band, lon_table, (((0,), (0,)), ((), ())), precision=HIGHEST)
    return field.reshape(hours_dev, lat_dev, lon_size)


LANES = 128
ROWS = 8
MESH = pl.DeviceIdType.MESH
NT = (((1,), (1,)), ((), ()))
NN = (((1,), (0,)), ((), ()))


def round_up(value, unit):
    return -(-value // unit) * unit


def lon_tables(lon_size, times, bands, slots_used):
    half = lon_size // 2
    modes_dev = lon_size // bands
    slots = modes_dev // times
    mode = (
        np.arange(bands)[None, :, None] * modes_dev
        + np.arange(times)[:, None, None]
        + times * np.arange(slots)[None, None, :]
    )
    sine = mode > half
    frequency = np.where(sine, mode - half, mode)
    radians = (frequency[..., None] * np.arange(half) % lon_size) * (2.0 * math.pi / lon_size)
    waveform = np.where(sine[..., None], np.sin(radians), np.cos(radians))
    edge = (mode == 0) | (mode == half)
    table = waveform * np.where(edge, math.sqrt(1.0 / lon_size), math.sqrt(2.0 / lon_size))[..., None]
    full = np.zeros((times, bands, slots_used, round_up(half, LANES)), np.float32)
    full[:, :, :slots, :half] = table
    high = full.astype(jnp.bfloat16)
    low = (full - high.astype(np.float32)).astype(jnp.bfloat16)
    return high, low


def lat_tables(lat_size, bands):
    lat_dev = lat_size // bands
    wavenumber = np.arange(lat_size)[:, None]
    latitude = np.arange(lat_size)[None, :]
    radians = (wavenumber * (2 * latitude + 1) % (4 * lat_size)) * (math.pi / (2.0 * lat_size))
    table = np.cos(radians) * np.where(wavenumber == 0, math.sqrt(1.0 / lat_size), math.sqrt(2.0 / lat_size))
    full = np.zeros((lat_size, bands, ROWS), np.float32)
    full[:, :, :lat_dev] = table.reshape(lat_size, bands, lat_dev)
    full = full.reshape(lat_size, bands * ROWS)

    def stacked(array):
        high = array.astype(jnp.bfloat16)
        return np.concatenate([high, (array - high.astype(np.float32)).astype(jnp.bfloat16)], axis=0)

    return stacked(full), stacked(np.ascontiguousarray(full.T))


def split(value):
    high = value.astype(jnp.bfloat16)
    low = (value - high.astype(jnp.float32)).astype(jnp.bfloat16)
    return high, low


def paired_dot(table, value):
    both = jnp.concatenate(split(value), axis=1)
    product = lax.dot_general(table, both, NN, preferred_element_type=jnp.float32)
    rows = table.shape[0] // 2
    return product[:rows, :LANES] + (product[:rows, LANES:] + product[rows:, :LANES])


def swap_halves(first, second):
    left = lax.broadcasted_iota(jnp.int32, first.shape, 1) < LANES // 2
    return (
        jnp.where(left, first, pltpu.roll(second, LANES // 2, 1)),
        jnp.where(left, pltpu.roll(first, LANES // 2, 1), second),
    )


def symmetric_gains(noise_ref, variance, scale, transition_ref, gain_ref, smoother_ref):
    hours = gain_ref.shape[0]
    transition, stationary, process = model_terms(variance, scale)
    pairs = [(0, 0), (0, 1), (0, 2), (1, 1), (1, 2), (2, 2)]
    for row in range(3):
        for column in range(3):
            transition_ref[row, column] = transition[row][column]

    def unpack(packed):
        matrix = [[None] * 3 for _ in range(3)]
        for (row, column), value in zip(pairs, packed):
            matrix[row][column] = matrix[column][row] = value
        return matrix

    def update(predicted, hour):
        inverse_var = 1.0 / (predicted[0][0] + noise_ref[hour])
        gain = [predicted[row][0] * inverse_var for row in range(3)]
        for row in range(3):
            gain_ref[hour, row] = gain[row]
        return [predicted[row][column] - gain[row] * predicted[0][column] for row, column in pairs]

    def step(hour, packed):
        covariance = unpack(packed)
        moved = mat_mul(transition, covariance)
        predicted = unpack(
            [
                moved[row][0] * transition[column][0]
                + moved[row][1] * transition[column][1]
                + moved[row][2] * transition[column][2]
                + process[row][column]
                for row, column in pairs
            ]
        )
        c00 = predicted[1][1] * predicted[2][2] - predicted[1][2] * predicted[1][2]
        c01 = predicted[0][2] * predicted[1][2] - predicted[0][1] * predicted[2][2]
        c02 = predicted[0][1] * predicted[1][2] - predicted[0][2] * predicted[1][1]
        c11 = predicted[0][0] * predicted[2][2] - predicted[0][2] * predicted[0][2]
        c12 = predicted[0][1] * predicted[0][2] - predicted[0][0] * predicted[1][2]
        c22 = predicted[0][0] * predicted[1][1] - predicted[0][1] * predicted[0][1]
        inverse_det = 1.0 / (predicted[0][0] * c00 + predicted[0][1] * c01 + predicted[0][2] * c02)
        cofactors = unpack([c00, c01, c02, c11, c12, c22])
        for row in range(3):
            scaled = [moved[within][row] * inverse_det for within in range(3)]
            for column in range(3):
                smoother_ref[hour - 1, row, column] = (
                    scaled[0] * cofactors[0][column]
                    + scaled[1] * cofactors[1][column]
                    + scaled[2] * cofactors[2][column]
                )
        return tuple(update(predicted, hour))

    first = tuple(update(stationary, 0))
    lax.fori_loop(1, hours, step, first)


def smoother_kernel(
    times,
    bands,
    slots_used,
    observed_hbm,
    noise_hbm,
    variance_hbm,
    scale_hbm,
    forward_lat_hbm,
    inverse_lat_hbm,
    high_hbm,
    low_hbm,
    out_ref,
    observed_ref,
    noise_ref,
    variance_ref,
    scale_ref,
    forward_lat_ref,
    inverse_lat_ref,
    high,
    low,
    folded,
    outbox,
    inbox,
    outbox_back,
    inbox_back,
    transition_ref,
    gain_ref,
    smoother_ref,
    input_sem,
    table_sem,
    send_sem,
    recv_sem,
    send_back_sem,
    recv_back_sem,
):
    devices = times * bands
    stride = 5 if devices % 5 else 1
    my_time = lax.axis_index("tm")
    my_band = lax.axis_index("space")
    me = my_time * bands + my_band
    lat_dev, lon_size = observed_ref.shape[0], observed_ref.shape[2]
    half = lon_size // 2
    hours = gain_ref.shape[0]
    n_half = gain_ref.shape[2]
    width = LANES // 2

    def table_copy(time, which):
        source, target = ((high_hbm, high), (low_hbm, low))[which]
        return pltpu.make_async_copy(
            source.at[time], target.at[time, :, pl.ds(0, slots_used), :], table_sem.at[time, which]
        )

    inputs = [
        pltpu.make_async_copy(source, target, input_sem.at[index])
        for index, (source, target) in enumerate(
            [
                (observed_hbm, observed_ref),
                (noise_hbm, noise_ref),
                (variance_hbm, variance_ref),
                (scale_hbm, scale_ref),
                (forward_lat_hbm, forward_lat_ref),
                (inverse_lat_hbm, inverse_lat_ref),
            ]
        )
    ]
    inputs[0].start()
    for time in range(times):
        table_copy(time, 0).start()
        table_copy(time, 1).start()
    for copy in inputs[1:]:
        copy.start()

    inbox[...] = jnp.zeros_like(inbox)
    inbox_back[...] = jnp.zeros_like(inbox_back)

    barrier = pltpu.get_barrier_semaphore()

    def greet(step, carry):
        peer = lax.rem(me + step, devices)
        pl.semaphore_signal(
            barrier, inc=1, device_id=(peer // bands, lax.rem(peer, bands)), device_id_type=MESH
        )
        return carry

    lax.fori_loop(1, devices, greet, 0)

    spare = width - slots_used
    high[:, :, slots_used:, :] = jnp.zeros((times, bands, spare, high.shape[3]), high.dtype)
    low[:, :, slots_used:, :] = jnp.zeros((times, bands, spare, low.shape[3]), low.dtype)
    folded[...] = jnp.zeros_like(folded)
    inputs[0].wait()
    for hour in range(2):
        early = observed_ref[:, hour, :half]
        late = observed_ref[:, hour, half:]
        folded[0, hour * ROWS : hour * ROWS + lat_dev, :half] = early + late
        folded[1, hour * ROWS : hour * ROWS + lat_dev, :half] = early - late
    rows = []
    for parity in range(2):
        upper, lower = split(folded[parity])
        rows.append((jnp.concatenate([upper, lower], axis=0), upper))

    def flat(ref, time):
        return ref[time].reshape(bands * width, ref.shape[3])

    for time in range(times):
        table_copy(time, 0).wait()
        table_copy(time, 1).wait()
        both, upper = rows[time % 2]
        wide = lax.dot_general(both, flat(high, time), NT, preferred_element_type=jnp.float32)
        rest = lax.dot_general(upper, flat(low, time), NT, preferred_element_type=jnp.float32)
        spectra = wide[: 2 * ROWS] + wide[2 * ROWS :] + rest
        for pair in range(bands // 2):
            block = spectra[:, pair * LANES : (pair + 1) * LANES]
            owner = time * bands + 2 * pair
            outbox[owner], outbox[owner + 1] = swap_halves(block[:ROWS], block[ROWS:])

    pl.semaphore_wait(barrier, devices - 1)

    def exchange(box, landing, sends, recvs, peer, slot):
        return pltpu.make_async_remote_copy(
            src_ref=box.at[peer, pl.ds(0, lat_dev)],
            dst_ref=landing.at[slot, pl.ds(0, lat_dev)],
            send_sem=sends.at[0],
            recv_sem=recvs.at[slot // bands],
            device_id=(peer // bands, lax.rem(peer, bands)),
            device_id_type=MESH,
        )

    def send(step, carry):
        peer = lax.rem(me + step * stride, devices)
        exchange(outbox, inbox, send_sem, recv_sem, peer, me).start()
        return carry

    def sent(box, sends):
        gone = box.at[pl.ds(0, devices - 1), pl.ds(0, lat_dev)]
        pltpu.make_async_copy(gone, gone, sends.at[0]).wait()

    def arrive(landing, recvs, step):
        time = lax.rem(my_time + step, times)
        come = landing.at[pl.ds(0, bands - 1 if step == 0 else bands), pl.ds(0, lat_dev)]
        pltpu.make_async_copy(come, come, recvs.at[time]).wait()
        return time

    lax.fori_loop(1, devices, send, 0)
    inbox[me] = outbox[me]

    for copy in inputs[1:]:
        copy.wait()
    modes_dev = variance_ref.shape[1]
    slots = modes_dev // times
    mode = lax.broadcasted_iota(jnp.int32, (modes_dev, LANES), 0)
    slot = lax.rem(lax.broadcasted_iota(jnp.int32, (modes_dev, LANES), 1), width)
    picked = ((mode == slot * times + my_time) & (slot < slots)).astype(jnp.float32)
    tile_lane = lax.broadcasted_iota(jnp.int32, (n_half, LANES), 1)

    def own_modes(ref):
        mine = lax.dot_general(ref[...], picked, NN, precision=HIGHEST, preferred_element_type=jnp.float32)
        mine = jnp.where(tile_lane < width, mine[:n_half], mine[n_half:])
        return jnp.where(lax.rem(tile_lane, width) < slots, mine, 1.0)

    symmetric_gains(
        noise_ref, own_modes(variance_ref), own_modes(scale_ref), transition_ref, gain_ref, smoother_ref
    )
    for step in range(times):
        arrive(inbox, recv_sem, step)

    spectra = []
    for time in range(times):
        arrived = inbox[time * bands : (time + 1) * bands].reshape(bands * ROWS, LANES)
        mixed = paired_dot(forward_lat_ref[...], arrived)
        spectra.extend(swap_halves(mixed[:n_half], mixed[n_half:]))

    transition = [[transition_ref[row, column] for column in range(3)] for row in range(3)]
    means, predictions = [], [None]
    means.append([gain_ref[0, row] * spectra[0] for row in range(3)])
    for hour in range(1, hours):
        predicted = mat_vec(transition, means[-1])
        residual = spectra[hour] - predicted[0]
        predictions.append(predicted)
        means.append([predicted[row] + gain_ref[hour, row] * residual for row in range(3)])
    smoothed = means[-1]
    series = [None] * hours
    series[hours - 1] = smoothed[0]
    for hour in range(hours - 2, -1, -1):
        difference = [smoothed[row] - predictions[hour + 1][row] for row in range(3)]
        smoothed = [
            means[hour][row]
            + smoother_ref[hour, row, 0] * difference[0]
            + smoother_ref[hour, row, 1] * difference[1]
            + smoother_ref[hour, row, 2] * difference[2]
            for row in range(3)
        ]
        series[hour] = smoothed[0]

    for time in range(times):
        stacked = jnp.concatenate(swap_halves(series[2 * time], series[2 * time + 1]), axis=0)
        grid = paired_dot(inverse_lat_ref[...], stacked)
        outbox_back[time * bands : (time + 1) * bands] = grid.reshape(bands, ROWS, LANES)

    def send_back(step, carry):
        peer = lax.rem(me + step * stride, devices)
        exchange(outbox_back, inbox_back, send_back_sem, recv_back_sem, peer, me).start()
        return carry

    lax.fori_loop(1, devices, send_back, 0)
    inbox_back[me] = outbox_back[me]

    early = late = 0.0
    for step in range(times):
        time = arrive(inbox_back, recv_back_sem, step)
        blocks = []
        for pair in range(bands // 2):
            owner = time * bands + 2 * pair
            first, second = swap_halves(inbox_back[owner], inbox_back[owner + 1])
            blocks.append(jnp.concatenate([first, second], axis=0))
        upper, lower = split(jnp.concatenate(blocks, axis=1))
        both = jnp.concatenate([upper, lower], axis=0)
        wide = lax.dot_general(both, flat(high, time), NN, preferred_element_type=jnp.float32)
        rest = lax.dot_general(upper, flat(low, time), NN, preferred_element_type=jnp.float32)
        part = wide[: 2 * ROWS] + wide[2 * ROWS :] + rest
        early = early + part
        late = late + jnp.where(lax.rem(time, 2) == 0, part, -part)
    sent(outbox, send_sem)
    sent(outbox_back, send_back_sem)
    for hour in range(2):
        out_ref[:, hour, :half] = early[hour * ROWS : hour * ROWS + lat_dev, :half]
        out_ref[:, hour, half:] = late[hour * ROWS : hour * ROWS + lat_dev, :half]


def per_device_fused(observed, noise_var, spectral_var, time_scale):
    times, bands = lax.axis_size("tm"), lax.axis_size("space")
    hours_dev, lat_dev, lon_size = observed.shape
    hours, lat_size = noise_var.shape[0], spectral_var.shape[1]
    slots_used = round_up(spectral_var.shape[0] // times, 2 * ROWS)
    n_half, width = lat_size // 2, LANES // 2
    half_padded = round_up(lon_size // 2, LANES)

    high, low = lon_tables(lon_size, times, bands, slots_used)
    forward_lat, inverse_lat = lat_tables(lat_size, bands)
    in_vmem = pl.BlockSpec(memory_space=pltpu.VMEM)
    in_place = pl.BlockSpec(memory_space=pltpu.HBM)
    box = pltpu.VMEM((times * bands, ROWS, LANES), jnp.float32)
    table = pltpu.VMEM((times, bands, width, half_padded), jnp.bfloat16)
    dma = pltpu.SemaphoreType.DMA
    field = pl.pallas_call(
        functools.partial(smoother_kernel, times, bands, slots_used),
        out_shape=pltpu.VMEM((lat_dev, hours_dev, lon_size), jnp.float32),
        in_specs=[in_place] * 8,
        out_specs=in_vmem,
        scratch_shapes=[
            pltpu.VMEM((lat_dev, hours_dev, lon_size), jnp.float32),
            pltpu.SMEM((hours,), jnp.float32),
            pltpu.VMEM((lat_size, spectral_var.shape[0]), jnp.float32),
            pltpu.VMEM((lat_size, spectral_var.shape[0]), jnp.float32),
            pltpu.VMEM(forward_lat.shape, jnp.bfloat16),
            pltpu.VMEM(inverse_lat.shape, jnp.bfloat16),
            table,
            table,
            pltpu.VMEM((2, 2 * ROWS, half_padded), jnp.float32),
            box,
            box,
            box,
            box,
            pltpu.VMEM((3, 3, n_half, LANES), jnp.float32),
            pltpu.VMEM((hours, 3, n_half, LANES), jnp.float32),
            pltpu.VMEM((hours, 3, 3, n_half, LANES), jnp.float32),
            dma((6,)),
            dma((times, 2)),
            dma((1,)),
            dma((times,)),
            dma((1,)),
            dma((times,)),
        ],
        compiler_params=pltpu.CompilerParams(collective_id=0, has_side_effects=True),
    )(
        observed.transpose(1, 0, 2),
        noise_var,
        spectral_var.T,
        time_scale.T,
        jnp.asarray(forward_lat),
        jnp.asarray(inverse_lat),
        jnp.asarray(high),
        jnp.asarray(low),
    )
    return field.transpose(1, 0, 2)


def fits(observed, spectral_var):
    times, bands = lax.axis_size("tm"), lax.axis_size("space")
    hours_dev, lat_dev, lon_size = observed.shape
    modes_dev, lat_size = spectral_var.shape
    return (
        hours_dev == 2
        and lat_dev <= ROWS
        and lat_size % (2 * ROWS) == 0
        and bands % 2 == 0
        and times % 2 == 0
        and lon_size % 4 == 0
        and modes_dev % 2 == 0
        and modes_dev % times == 0
        and LANES // 4 < modes_dev // times <= LANES // 2
    )


def per_device(observed, noise_var, spectral_var, time_scale):
    if fits(observed, spectral_var):
        return per_device_fused(observed, noise_var, spectral_var, time_scale)
    return per_device_general(observed, noise_var, spectral_var, time_scale)


def solution(mesh):
    placed = (P("tm", "space", None), P(), P("space", None), P("space", None))
    return jax.shard_map(
        per_device, mesh=mesh, in_specs=placed, out_specs=P("tm", "space", None), check_vma=False
    )
```

profile of v0, /device:TPU:0, one launch (start us, length us, event | category | flops | bytes accessed | tf_op | source)
XLA Modules:
  0.0 19.7 jit_solution(1372688835925970417)
XLA Ops:
  0.0 19.0 %shard_map.82 = f32[6,2,1440]{2,1,0:T(2,128)S(1)} custom-call(f32[6,2,1440]{2,1,0:T(2,128)} %bitcast.5, f32[8]{0:T(128)} %noise_hbm.1, f32[48,180]{1,0:T(8,128)} %bitcast.6, f32[48,180]{1,0:T(8,128)} %bitcast.7, bf16[96,64]{1,0:T(8,128)(2,1)} %constant.8.clone.forward_lat_hbm, bf16[128,48]{1,0:T(8,128)(2,1)} %constant.9.clone.inverse_lat_hbm, ...), custom_call_target="tpu_custom_call" | custom-call | tf_op jit(solution)/shard_map/pallas_call | solution.py:574
  19.1 0.6 %copy.10 = f32[2,6,1440]{2,0,1:T(2,128)} copy(f32[2,6,1440]{2,0,1:T(2,128)S(1)} %bitcast.4) | data formatting | bytes 138240
where the time goes:
time: 19.9 us; the launch traced here: 19.7 us
  Pallas kernels  19 us (95%)
  local copies, waits for them, and re-layouts  0.64 us (3%)
    pallas_call x1, Pallas kernels, per_device_fused(): pl.pallas_call(functools.partial(smoother_kernel, times, bands, slots_use...  19 us
    unnamed x1, local copies, waits for them, and re-layouts  0.64 us

commit v1 on v0

--- a/solution.py
+++ b/solution.py
@@ -211,25 +211,80 @@
     return -(-value // unit) * unit
 
 
-def lon_tables(lon_size, times, bands, slots_used):
-    half = lon_size // 2
+KINDS = 3
+WIDTH = LANES // 2
+QUARTER = LANES // 4
+
+
+def hops(time, band, times, bands):
+    wide = math.isqrt(bands // 2)
+    return time // 2 + band // wide + band % wide
+
+
+def plan(times, bands):
+    cosines = bands // 2
+    jobs = [
+        (band, kind)
+        for base in (0, cosines)
+        for kind in range(KINDS)
+        for band in range(base, base + cosines)
+    ]
+    devices = [(time, band) for time in range(times) for band in range(bands)]
+    chosen = sorted(devices, key=lambda d: (hops(*d, times, bands), d))[: len(jobs)]
+    owner, free = {}, []
+    for band in range(bands):
+        local = sorted(d for d in chosen if d[1] == band)
+        for kind, device in enumerate(local[:KINDS]):
+            owner[band, kind] = device
+        free.extend(local[KINDS:])
+    free.sort(key=lambda d: -hops(*d, times, bands))
+    sources, used = {}, {}
+    for job in jobs:
+        if job not in owner:
+            owner[job] = free.pop(0)
+            sources[job] = (used.get(job[0], 0), job[0])
+            used[job[0]] = sources[job][0] + 1
+    return jobs, [owner[job] for job in jobs], [sources.get(job) for job in jobs]
+
+
+def mode_columns(modes_dev):
+    full = modes_dev // KINDS
+    return full, modes_dev // 2 - full
+
+
+def lon_tables(lon_size, bands):
+    half, cosines = lon_size // 2, bands // 2
     modes_dev = lon_size // bands
-    slots = modes_dev // times
-    mode = (
-        np.arange(bands)[None, :, None] * modes_dev
-        + np.arange(times)[:, None, None]
-        + times * np.arange(slots)[None, None, :]
-    )
-    sine = mode > half
-    frequency = np.where(sine, mode - half, mode)
-    radians = (frequency[..., None] * np.arange(half) % lon_size) * (2.0 * math.pi / lon_size)
-    waveform = np.where(sine[..., None], np.sin(radians), np.cos(radians))
-    edge = (mode == 0) | (mode == half)
-    table = waveform * np.where(edge, math.sqrt(1.0 / lon_size), math.sqrt(2.0 / lon_size))[..., None]
-    full = np.zeros((times, bands, slots_used, round_up(half, LANES)), np.float32)
-    full[:, :, :slots, :half] = table
-    high = full.astype(jnp.bfloat16)
-    low = (full - high.astype(np.float32)).astype(jnp.bfloat16)
+    full, rest = mode_columns(modes_dev)
+    points = lon_size // 4 + 1
+    padded = round_up(points, LANES)
+    tables = np.zeros((4, cosines * (WIDTH + QUARTER), padded), np.float64)
+
+    def fill(kind, column, mode):
+        frequency = mode - half if mode > half else mode
+        radians = (frequency * np.arange(points) % lon_size) * (2.0 * math.pi / lon_size)
+        wave = np.sin(radians) if mode > half else np.cos(radians)
+        wave = wave * math.sqrt((1.0 if mode in (0, half) else 2.0) / lon_size)
+        wave[-1] *= 0.5
+        tables[kind, column, :points] = wave
+
+    for band in range(bands):
+        for parity in range(2):
+            kind = 2 * (band // cosines) + parity
+            for index in range(full + rest):
+                mode = band * modes_dev + 2 * index + parity
+                local = band % cosines
+                if index < full:
+                    column = local * WIDTH + index
+                else:
+                    column = cosines * WIDTH + local * QUARTER + index - full
+                if mode == half:
+                    fill(0, WIDTH - 1, mode)
+                else:
+                    fill(kind, column, mode)
+    tables = tables.astype(np.float32)
+    high = tables.astype(jnp.bfloat16)
+    low = (tables - high.astype(np.float32)).astype(jnp.bfloat16)
     return high, low
 
 
@@ -329,7 +384,6 @@
 def smoother_kernel(
     times,
     bands,
-    slots_used,
     observed_hbm,
     noise_hbm,
     variance_hbm,
@@ -352,6 +406,8 @@
     inbox,
     outbox_back,
     inbox_back,
+    params_out,
+    params,
     transition_ref,
     gain_ref,
     smoother_ref,
@@ -361,9 +417,14 @@
     recv_sem,
     send_back_sem,
     recv_back_sem,
+    params_send_sem,
+    params_recv_sem,
 ):
     devices = times * bands
+    cosines = bands // 2
     stride = 5 if devices % 5 else 1
+    jobs, owners, sources = plan(times, bands)
+    codes = [time * bands + band for time, band in owners]
     my_time = lax.axis_index("tm")
     my_band = lax.axis_index("space")
     me = my_time * bands + my_band
@@ -371,208 +432,375 @@
     half = lon_size // 2
     hours = gain_ref.shape[0]
     n_half = gain_ref.shape[2]
-    width = LANES // 2
-
-    def table_copy(time, which):
+    modes_dev = variance_ref.shape[1]
+    full, rest = mode_columns(modes_dev)
+    points = high.shape[2]
+    mirror = half % LANES
+
+    def pick(index, values):
+        total = 0
+        for place, value in enumerate(values):
+            total = total + jnp.where(index == place, value, 0)
+        return total
+
+    def mine(places, values):
+        total = 0
+        for place, value in zip(places, values):
+            total = total + jnp.where(me == place, value, 0)
+        return total
+
+    my_job = mine(codes, range(1, len(jobs) + 1)) - 1
+    owning = my_job >= 0
+    moved = [index for index, source in enumerate(sources) if source is not None]
+    source_codes = [sources[index][0] * bands + sources[index][1] for index in moved]
+    lending = mine(source_codes, [1] * len(moved)) > 0
+    borrowing = mine([codes[index] for index in moved], [1] * len(moved)) > 0
+
+    def table_copy(kind, which):
         source, target = ((high_hbm, high), (low_hbm, low))[which]
-        return pltpu.make_async_copy(
-            source.at[time], target.at[time, :, pl.ds(0, slots_used), :], table_sem.at[time, which]
-        )
+        return pltpu.make_async_copy(source.at[kind], target.at[kind], table_sem.at[kind, which])
 
     inputs = [
         pltpu.make_async_copy(source, target, input_sem.at[index])
         for index, (source, target) in enumerate(
             [
                 (observed_hbm, observed_ref),
-                (noise_hbm, noise_ref),
                 (variance_hbm, variance_ref),
                 (scale_hbm, scale_ref),
+                (noise_hbm, noise_ref),
                 (forward_lat_hbm, forward_lat_ref),
                 (inverse_lat_hbm, inverse_lat_ref),
             ]
         )
     ]
     inputs[0].start()
-    for time in range(times):
-        table_copy(time, 0).start()
-        table_copy(time, 1).start()
+    inbox[...] = jnp.zeros_like(inbox)
+    inbox_back[...] = jnp.zeros_like(inbox_back)
+
+    barrier = pltpu.get_barrier_semaphore()
+
+    @pl.when(owning)
+    def _():
+        def greet(step, carry):
+            peer = lax.rem(me + step, devices)
+            pl.semaphore_signal(
+                barrier, inc=1, device_id=(peer // bands, lax.rem(peer, bands)), device_id_type=MESH
+            )
+            return carry
+
+        lax.fori_loop(1, devices, greet, 0)
+
+    for kind in range(4):
+        table_copy(kind, 0).start()
+        table_copy(kind, 1).start()
     for copy in inputs[1:]:
         copy.start()
 
-    inbox[...] = jnp.zeros_like(inbox)
-    inbox_back[...] = jnp.zeros_like(inbox_back)
-
-    barrier = pltpu.get_barrier_semaphore()
-
-    def greet(step, carry):
-        peer = lax.rem(me + step, devices)
-        pl.semaphore_signal(
-            barrier, inc=1, device_id=(peer // bands, lax.rem(peer, bands)), device_id_type=MESH
-        )
-        return carry
-
-    lax.fori_loop(1, devices, greet, 0)
-
-    spare = width - slots_used
-    high[:, :, slots_used:, :] = jnp.zeros((times, bands, spare, high.shape[3]), high.dtype)
-    low[:, :, slots_used:, :] = jnp.zeros((times, bands, spare, low.shape[3]), low.dtype)
+    def own_modes(ref, kind):
+        mode = lax.broadcasted_iota(jnp.int32, (modes_dev, LANES), 0)
+        slot = lax.rem(lax.broadcasted_iota(jnp.int32, (modes_dev, LANES), 1), WIDTH)
+        second = (slot >= QUARTER).astype(jnp.int32)
+        place = slot - second * QUARTER
+        whole = jnp.where(slot < full, 2 * slot + kind, modes_dev)
+        mixed = jnp.where(place < rest, 2 * (full + place) + second, modes_dev)
+        wanted = jnp.where(kind == KINDS - 1, mixed, whole)
+        picked = (mode == wanted).astype(jnp.float32)
+        lane = lax.broadcasted_iota(jnp.int32, (n_half, LANES), 1)
+        used = wanted[:n_half] < modes_dev
+        value = lax.dot_general(ref[...], picked, NN, precision=HIGHEST, preferred_element_type=jnp.float32)
+        value = jnp.where(lane < WIDTH, value[:n_half], value[n_half:])
+        return jnp.where(used, value, 1.0)
+
     folded[...] = jnp.zeros_like(folded)
     inputs[0].wait()
+    lane = lax.broadcasted_iota(jnp.int32, (ROWS, LANES), 1)
+    reverse = lax.rem(mirror + LANES - lane, LANES)
+    straight = lane <= mirror
+
+    def flipped(value):
+        return jnp.take_along_axis(value, reverse, axis=1, mode="promise_in_bounds")
+
+    def tile(value, index):
+        return value[:, index * LANES : (index + 1) * LANES]
+
+    last = half // LANES
+    classes = [[], [], [], []]
     for hour in range(2):
         early = observed_ref[:, hour, :half]
         late = observed_ref[:, hour, half:]
-        folded[0, hour * ROWS : hour * ROWS + lat_dev, :half] = early + late
-        folded[1, hour * ROWS : hour * ROWS + lat_dev, :half] = early - late
-    rows = []
-    for parity in range(2):
-        upper, lower = split(folded[parity])
-        rows.append((jnp.concatenate([upper, lower], axis=0), upper))
-
-    def flat(ref, time):
-        return ref[time].reshape(bands * width, ref.shape[3])
-
-    for time in range(times):
-        table_copy(time, 0).wait()
-        table_copy(time, 1).wait()
-        both, upper = rows[time % 2]
-        wide = lax.dot_general(both, flat(high, time), NT, preferred_element_type=jnp.float32)
-        rest = lax.dot_general(upper, flat(low, time), NT, preferred_element_type=jnp.float32)
-        spectra = wide[: 2 * ROWS] + wide[2 * ROWS :] + rest
-        for pair in range(bands // 2):
-            block = spectra[:, pair * LANES : (pair + 1) * LANES]
-            owner = time * bands + 2 * pair
-            outbox[owner], outbox[owner + 1] = swap_halves(block[:ROWS], block[ROWS:])
-
-    pl.semaphore_wait(barrier, devices - 1)
-
-    def exchange(box, landing, sends, recvs, peer, slot):
+        folded[0, hour, :lat_dev, :half] = early + late
+        folded[1, hour, :lat_dev, :half] = early - late
+        for parity in range(2):
+            ahead = folded[parity, hour]
+            turned = {index: flipped(tile(ahead, index)) for index in range(last - points // LANES, last + 1)}
+            behind = jnp.concatenate(
+                [
+                    jnp.where(straight, turned[last - index], turned[last - index - 1])
+                    for index in range(points // LANES)
+                ],
+                axis=1,
+            )
+            ahead = ahead[:, :points]
+            classes[parity].append(ahead + behind if parity == 0 else ahead - behind)
+            classes[2 + parity].append(ahead - behind if parity == 0 else ahead + behind)
+
+    wide_lanes = cosines * WIDTH
+
+    def forward(kind):
+        table_copy(kind, 0).wait()
+        table_copy(kind, 1).wait()
+        upper, lower = split(jnp.concatenate(classes[kind], axis=0))
+        both = jnp.concatenate([upper, lower], axis=0)
+        wide = lax.dot_general(both, high[kind], NT, preferred_element_type=jnp.float32)
+        fine = lax.dot_general(upper, low[kind], NT, preferred_element_type=jnp.float32)
+        return wide[: 2 * ROWS] + wide[2 * ROWS :] + fine
+
+    def spin(value, amount):
+        amount = amount % LANES
+        return pltpu.roll(value, amount, 1) if amount else value
+
+    quarter = lane // QUARTER
+    middle = None
+    for side in range(2):
+        found = [forward(2 * side), forward(2 * side + 1)]
+        base = side * KINDS * cosines
+        for parity in range(2):
+            for pair in range(cosines // 2):
+                block = tile(found[parity], pair)
+                first, second = swap_halves(block[:ROWS], block[ROWS:])
+                if side == 0 and parity == 0 and pair == 0:
+                    middle = spin(first, 1)
+                if side == 1 and parity == 0 and pair == 0:
+                    first = jnp.where(lax.rem(lane, WIDTH) == 0, pltpu.roll(middle, WIDTH, 1), first)
+                outbox[base + parity * cosines + 2 * pair] = first
+                outbox[base + parity * cosines + 2 * pair + 1] = second
+        mixed = [value[:, wide_lanes:] for value in found]
+        for local in range(cosines):
+            parts = [
+                spin(mixed[part % 2][(part // 2) * ROWS : (part // 2 + 1) * ROWS], (part - local) * QUARTER)
+                for part in range(4)
+            ]
+            merged = jnp.where(quarter == 0, parts[0], parts[1])
+            merged = jnp.where(quarter == 2, parts[2], merged)
+            outbox[base + 2 * cosines + local] = jnp.where(quarter == 3, parts[3], merged)
+
+    inputs[1].wait()
+    inputs[2].wait()
+
+    @pl.when(lending)
+    def _():
+        kind = mine(source_codes, [jobs[index][1] for index in moved])
+        params_out[0] = own_modes(variance_ref, kind)
+        params_out[1] = own_modes(scale_ref, kind)
+
+    @pl.when(owning)
+    def _():
+        kind = mine(codes, [kind for _, kind in jobs])
+
+        @pl.when(jnp.logical_not(borrowing))
+        def _():
+            params[0] = own_modes(variance_ref, kind)
+            params[1] = own_modes(scale_ref, kind)
+
+    pl.semaphore_wait(barrier, len(jobs) - owning.astype(jnp.int32))
+
+    def params_copy():
+        target = mine(source_codes, [codes[index] for index in moved])
         return pltpu.make_async_remote_copy(
-            src_ref=box.at[peer, pl.ds(0, lat_dev)],
-            dst_ref=landing.at[slot, pl.ds(0, lat_dev)],
+            src_ref=params_out,
+            dst_ref=params,
+            send_sem=params_send_sem.at[0],
+            recv_sem=params_recv_sem.at[0],
+            device_id=(target // bands, lax.rem(target, bands)),
+            device_id_type=MESH,
+        )
+
+    @pl.when(lending)
+    def _():
+        params_copy().start()
+
+    def exchange(box, landing, sends, recv, slot, peer, target):
+        return pltpu.make_async_remote_copy(
+            src_ref=box.at[slot, pl.ds(0, lat_dev)],
+            dst_ref=landing.at[target, pl.ds(0, lat_dev)],
             send_sem=sends.at[0],
-            recv_sem=recvs.at[slot // bands],
+            recv_sem=recv,
             device_id=(peer // bands, lax.rem(peer, bands)),
             device_id_type=MESH,
         )
 
-    def send(step, carry):
-        peer = lax.rem(me + step * stride, devices)
-        exchange(outbox, inbox, send_sem, recv_sem, peer, me).start()
-        return carry
-
-    def sent(box, sends):
-        gone = box.at[pl.ds(0, devices - 1), pl.ds(0, lat_dev)]
-        pltpu.make_async_copy(gone, gone, sends.at[0]).wait()
-
-    def arrive(landing, recvs, step):
-        time = lax.rem(my_time + step, times)
-        come = landing.at[pl.ds(0, bands - 1 if step == 0 else bands), pl.ds(0, lat_dev)]
-        pltpu.make_async_copy(come, come, recvs.at[time]).wait()
-        return time
-
-    lax.fori_loop(1, devices, send, 0)
-    inbox[me] = outbox[me]
-
-    for copy in inputs[1:]:
+    def keep(box, landing, recv, slot, target):
+        return pltpu.make_async_copy(
+            box.at[slot, pl.ds(0, lat_dev)], landing.at[target, pl.ds(0, lat_dev)], recv
+        )
+
+    def landed(landing, recv, first, count):
+        come = landing.at[pl.ds(first, count), pl.ds(0, lat_dev)]
+        pltpu.make_async_copy(come, come, recv).wait()
+
+    for group in range(2 * KINDS):
+        for step in range(cosines):
+            local = lax.rem(me + step, cosines)
+            peer = pick(local, codes[group * cosines : (group + 1) * cosines])
+
+            @pl.when(peer != me)
+            def _():
+                exchange(outbox, inbox, send_sem, recv_sem.at[my_time], group * cosines + local, peer, me).start()
+
+    @pl.when(owning)
+    def _():
+        keep(outbox, inbox, recv_sem.at[my_time], my_job, me).start()
+
+    for copy in inputs[3:]:
         copy.wait()
-    modes_dev = variance_ref.shape[1]
-    slots = modes_dev // times
-    mode = lax.broadcasted_iota(jnp.int32, (modes_dev, LANES), 0)
-    slot = lax.rem(lax.broadcasted_iota(jnp.int32, (modes_dev, LANES), 1), width)
-    picked = ((mode == slot * times + my_time) & (slot < slots)).astype(jnp.float32)
-    tile_lane = lax.broadcasted_iota(jnp.int32, (n_half, LANES), 1)
-
-    def own_modes(ref):
-        mine = lax.dot_general(ref[...], picked, NN, precision=HIGHEST, preferred_element_type=jnp.float32)
-        mine = jnp.where(tile_lane < width, mine[:n_half], mine[n_half:])
-        return jnp.where(lax.rem(tile_lane, width) < slots, mine, 1.0)
-
-    symmetric_gains(
-        noise_ref, own_modes(variance_ref), own_modes(scale_ref), transition_ref, gain_ref, smoother_ref
-    )
-    for step in range(times):
-        arrive(inbox, recv_sem, step)
-
-    spectra = []
-    for time in range(times):
-        arrived = inbox[time * bands : (time + 1) * bands].reshape(bands * ROWS, LANES)
-        mixed = paired_dot(forward_lat_ref[...], arrived)
-        spectra.extend(swap_halves(mixed[:n_half], mixed[n_half:]))
-
-    transition = [[transition_ref[row, column] for column in range(3)] for row in range(3)]
-    means, predictions = [], [None]
-    means.append([gain_ref[0, row] * spectra[0] for row in range(3)])
-    for hour in range(1, hours):
-        predicted = mat_vec(transition, means[-1])
-        residual = spectra[hour] - predicted[0]
-        predictions.append(predicted)
-        means.append([predicted[row] + gain_ref[hour, row] * residual for row in range(3)])
-    smoothed = means[-1]
-    series = [None] * hours
-    series[hours - 1] = smoothed[0]
-    for hour in range(hours - 2, -1, -1):
-        difference = [smoothed[row] - predictions[hour + 1][row] for row in range(3)]
-        smoothed = [
-            means[hour][row]
-            + smoother_ref[hour, row, 0] * difference[0]
-            + smoother_ref[hour, row, 1] * difference[1]
-            + smoother_ref[hour, row, 2] * difference[2]
-            for row in range(3)
-        ]
-        series[hour] = smoothed[0]
-
-    for time in range(times):
-        stacked = jnp.concatenate(swap_halves(series[2 * time], series[2 * time + 1]), axis=0)
-        grid = paired_dot(inverse_lat_ref[...], stacked)
-        outbox_back[time * bands : (time + 1) * bands] = grid.reshape(bands, ROWS, LANES)
-
-    def send_back(step, carry):
-        peer = lax.rem(me + step * stride, devices)
-        exchange(outbox_back, inbox_back, send_back_sem, recv_back_sem, peer, me).start()
-        return carry
-
-    lax.fori_loop(1, devices, send_back, 0)
-    inbox_back[me] = outbox_back[me]
-
-    early = late = 0.0
-    for step in range(times):
-        time = arrive(inbox_back, recv_back_sem, step)
-        blocks = []
-        for pair in range(bands // 2):
-            owner = time * bands + 2 * pair
-            first, second = swap_halves(inbox_back[owner], inbox_back[owner + 1])
-            blocks.append(jnp.concatenate([first, second], axis=0))
-        upper, lower = split(jnp.concatenate(blocks, axis=1))
+
+    @pl.when(owning)
+    def _():
+        @pl.when(borrowing)
+        def _():
+            pltpu.make_async_copy(params, params, params_recv_sem.at[0]).wait()
+
+        symmetric_gains(noise_ref, params[0], params[1], transition_ref, gain_ref, smoother_ref)
+
+        spectra = []
+        for time in range(times):
+            landed(inbox, recv_sem.at[time], time * bands, bands)
+            arrived = inbox[time * bands : (time + 1) * bands].reshape(bands * ROWS, LANES)
+            mixed = paired_dot(forward_lat_ref[...], arrived)
+            spectra.extend(swap_halves(mixed[:n_half], mixed[n_half:]))
+
+        transition = [[transition_ref[row, column] for column in range(3)] for row in range(3)]
+        means, predictions = [], [None]
+        means.append([gain_ref[0, row] * spectra[0] for row in range(3)])
+        for hour in range(1, hours):
+            predicted = mat_vec(transition, means[-1])
+            residual = spectra[hour] - predicted[0]
+            predictions.append(predicted)
+            means.append([predicted[row] + gain_ref[hour, row] * residual for row in range(3)])
+        smoothed = means[-1]
+        series = [None] * hours
+        series[hours - 1] = smoothed[0]
+        for hour in range(hours - 2, -1, -1):
+            difference = [smoothed[row] - predictions[hour + 1][row] for row in range(3)]
+            smoothed = [
+                means[hour][row]
+                + smoother_ref[hour, row, 0] * difference[0]
+                + smoother_ref[hour, row, 1] * difference[1]
+                + smoother_ref[hour, row, 2] * difference[2]
+                for row in range(3)
+            ]
+            series[hour] = smoothed[0]
+
+        for time in range(times):
+            stacked = jnp.concatenate(swap_halves(series[2 * time], series[2 * time + 1]), axis=0)
+            grid = paired_dot(inverse_lat_ref[...], stacked)
+            outbox_back[time * bands : (time + 1) * bands] = grid.reshape(bands, ROWS, LANES)
+
+        def send_back(step, carry):
+            peer = lax.rem(me + step * stride, devices)
+            exchange(
+                outbox_back, inbox_back, send_back_sem, recv_back_sem.at[my_job // cosines], peer, peer, my_job
+            ).start()
+            return carry
+
+        lax.fori_loop(1, devices, send_back, 0)
+        keep(outbox_back, inbox_back, recv_back_sem.at[my_job // cosines], me, my_job).start()
+
+    sums = []
+    later = None
+    for side in range(2):
+        base = side * KINDS * cosines
+        boxes = {}
+        for group in ((2, 0, 1) if side == 0 else (0, 2, 1)):
+            landed(inbox_back, recv_back_sem.at[side * KINDS + group], base + group * cosines, cosines)
+            for local in range(cosines):
+                boxes[group, local] = inbox_back[base + group * cosines + local]
+        shared = [[], []]
+        for hour in range(2):
+            for parity in range(2):
+                merged = None
+                for local in range(cosines):
+                    moved_part = spin(boxes[2, local], (local - (2 * hour + parity)) * QUARTER)
+                    merged = moved_part if merged is None else jnp.where(quarter == local, moved_part, merged)
+                shared[parity].append(merged)
+        for parity in range(2):
+            blocks = []
+            for pair in range(cosines // 2):
+                first, second = swap_halves(boxes[parity, 2 * pair], boxes[parity, 2 * pair + 1])
+                blocks.append([first, second])
+            blocks.append(shared[parity])
+            sums.append(blocks)
+    origin = inbox_back[KINDS * cosines]
+    for hour in range(2):
+        shift = WIDTH - 1 - hour * WIDTH
+        sums[0][0][hour] = jnp.where(lane == WIDTH - 1, spin(origin, shift), sums[0][0][hour])
+
+    grids = []
+    for kind in range(4):
+        upper, lower = split(
+            jnp.concatenate([jnp.concatenate(block, axis=0) for block in sums[kind]], axis=1)
+        )
         both = jnp.concatenate([upper, lower], axis=0)
-        wide = lax.dot_general(both, flat(high, time), NN, preferred_element_type=jnp.float32)
-        rest = lax.dot_general(upper, flat(low, time), NN, preferred_element_type=jnp.float32)
-        part = wide[: 2 * ROWS] + wide[2 * ROWS :] + rest
-        early = early + part
-        late = late + jnp.where(lax.rem(time, 2) == 0, part, -part)
-    sent(outbox, send_sem)
-    sent(outbox_back, send_back_sem)
+        wide = lax.dot_general(both, high[kind], NN, preferred_element_type=jnp.float32)
+        fine = lax.dot_general(upper, low[kind], NN, preferred_element_type=jnp.float32)
+        grids.append(wide[: 2 * ROWS] + wide[2 * ROWS :] + fine)
+
+    count = points // LANES
     for hour in range(2):
-        out_ref[:, hour, :half] = early[hour * ROWS : hour * ROWS + lat_dev, :half]
-        out_ref[:, hour, half:] = late[hour * ROWS : hour * ROWS + lat_dev, :half]
+        even_cos, odd_cos, even_sin, odd_sin = [grid[hour * ROWS : (hour + 1) * ROWS] for grid in grids]
+        ahead, ahead_odd = even_cos + even_sin, odd_cos + odd_sin
+        behind, behind_odd = even_cos - even_sin, odd_sin - odd_cos
+        for side in range(2):
+            start = ahead + ahead_odd if side == 0 else ahead - ahead_odd
+            end = behind + behind_odd if side == 0 else behind - behind_odd
+            turned = [flipped(tile(end, index)) for index in range(count)]
+            pieces = [tile(start, index) for index in range(count - 1)]
+            border = half // 2 - (count - 1) * LANES
+            fold = tile(start, count - 1)
+            fold = jnp.where(lane == border, fold + fold, fold)
+            pieces.append(jnp.where(lane <= border, fold, turned[count - 1]))
+            for index in range(count - 1, 0, -1):
+                pieces.append(jnp.where(straight, turned[index], turned[index - 1]))
+            pieces.append(turned[0])
+            row = jnp.concatenate(pieces, axis=1)
+            out_ref[:, hour, side * half : (side + 1) * half] = row[:lat_dev, :half]
+
+    def gone(box, sends, count):
+        left = box.at[pl.ds(0, count), pl.ds(0, lat_dev)]
+        pltpu.make_async_copy(left, left, sends.at[0]).wait()
+
+    gone(outbox, send_sem, len(jobs) - 1)
+
+    @pl.when(jnp.logical_not(owning))
+    def _():
+        gone(outbox, send_sem, 1)
+
+    @pl.when(owning)
+    def _():
+        gone(outbox_back, send_back_sem, devices - 1)
+
+    @pl.when(lending)
+    def _():
+        pltpu.make_async_copy(params_out, params_out, params_send_sem.at[0]).wait()
 
 
 def per_device_fused(observed, noise_var, spectral_var, time_scale):
     times, bands = lax.axis_size("tm"), lax.axis_size("space")
     hours_dev, lat_dev, lon_size = observed.shape
     hours, lat_size = noise_var.shape[0], spectral_var.shape[1]
-    slots_used = round_up(spectral_var.shape[0] // times, 2 * ROWS)
-    n_half, width = lat_size // 2, LANES // 2
+    n_half = lat_size // 2
     half_padded = round_up(lon_size // 2, LANES)
-
-    high, low = lon_tables(lon_size, times, bands, slots_used)
+    n_jobs = KINDS * bands
+
+    high, low = lon_tables(lon_size, bands)
     forward_lat, inverse_lat = lat_tables(lat_size, bands)
     in_vmem = pl.BlockSpec(memory_space=pltpu.VMEM)
     in_place = pl.BlockSpec(memory_space=pltpu.HBM)
     box = pltpu.VMEM((times * bands, ROWS, LANES), jnp.float32)
-    table = pltpu.VMEM((times, bands, width, half_padded), jnp.bfloat16)
+    job_box = pltpu.VMEM((n_jobs, ROWS, LANES), jnp.float32)
     dma = pltpu.SemaphoreType.DMA
     field = pl.pallas_call(
-        functools.partial(smoother_kernel, times, bands, slots_used),
+        functools.partial(smoother_kernel, times, bands),
         out_shape=pltpu.VMEM((lat_dev, hours_dev, lon_size), jnp.float32),
         in_specs=[in_place] * 8,
         out_specs=in_vmem,
@@ -583,22 +811,26 @@
             pltpu.VMEM((lat_size, spectral_var.shape[0]), jnp.float32),
             pltpu.VMEM(forward_lat.shape, jnp.bfloat16),
             pltpu.VMEM(inverse_lat.shape, jnp.bfloat16),
-            table,
-            table,
-            pltpu.VMEM((2, 2 * ROWS, half_padded), jnp.float32),
+            pltpu.VMEM(high.shape, jnp.bfloat16),
+            pltpu.VMEM(low.shape, jnp.bfloat16),
+            pltpu.VMEM((2, 2, ROWS, half_padded), jnp.float32),
+            job_box,
             box,
             box,
-            box,
-            box,
+            job_box,
+            pltpu.VMEM((2, n_half, LANES), jnp.float32),
+            pltpu.VMEM((2, n_half, LANES), jnp.float32),
             pltpu.VMEM((3, 3, n_half, LANES), jnp.float32),
             pltpu.VMEM((hours, 3, n_half, LANES), jnp.float32),
             pltpu.VMEM((hours, 3, 3, n_half, LANES), jnp.float32),
             dma((6,)),
-            dma((times, 2)),
+            dma((4, 2)),
             dma((1,)),
             dma((times,)),
             dma((1,)),
-            dma((times,)),
+            dma((2 * KINDS,)),
+            dma((1,)),
+            dma((1,)),
         ],
         compiler_params=pltpu.CompilerParams(collective_id=0, has_side_effects=True),
     )(
@@ -618,16 +850,23 @@
     times, bands = lax.axis_size("tm"), lax.axis_size("space")
     hours_dev, lat_dev, lon_size = observed.shape
     modes_dev, lat_size = spectral_var.shape
+    full, rest = mode_columns(modes_dev)
+    half, points = lon_size // 2, round_up(lon_size // 4 + 1, LANES)
     return (
         hours_dev == 2
         and lat_dev <= ROWS
         and lat_size % (2 * ROWS) == 0
-        and bands % 2 == 0
-        and times % 2 == 0
+        and times == KINDS + 1
+        and 2 * math.isqrt(bands // 2) ** 2 == bands
+        and bands == LANES // 16
         and lon_size % 4 == 0
         and modes_dev % 2 == 0
-        and modes_dev % times == 0
-        and LANES // 4 < modes_dev // times <= LANES // 2
+        and modes_dev % KINDS == 0
+        and full < WIDTH
+        and rest <= QUARTER
+        and half % LANES > 0
+        and round_up(half, LANES) == 2 * points
+        and half // 2 >= points - LANES
     )
 
 

time: 19.9 us -> 18.5 us (0.930)
  Pallas kernels: 19 us -> 17.7 us
    pallas_call x1, Pallas kernels: 19 us -> 17.7 us  [per_device_fused(): pl.pallas_call(functools.partial(smoother_kernel, times, bands), out_shap...]
where the time goes in v1:
time: 18.5 us; the launch traced here: 18.3 us
  Pallas kernels  17.7 us (96%)
  local copies, waits for them, and re-layouts  0.64 us (3%)
    pallas_call x1, Pallas kernels, per_device_fused(): pl.pallas_call(functools.partial(smoother_kernel, times, bands), out_shap...  17.7 us
    unnamed x1, local copies, waits for them, and re-layouts  0.64 us

profile of v1, /device:TPU:0, one launch (start us, length us, event | category | flops | bytes accessed | tf_op | source)
XLA Modules:
  0.0 18.3 jit_solution(7294651193737612892)
XLA Ops:
  0.0 17.7 %shard_map.82 = f32[6,2,1440]{2,1,0:T(2,128)S(1)} custom-call(f32[6,2,1440]{2,1,0:T(2,128)} %bitcast.5, f32[8]{0:T(128)} %noise_hbm.1, f32[48,180]{1,0:T(8,128)} %bitcast.6, f32[48,180]{1,0:T(8,128)} %bitcast.7, bf16[96,64]{1,0:T(8,128)(2,1)} %constant.8.clone.forward_lat_hbm, bf16[128,48]{1,0:T(8,128)(2,1)} %constant.9.clone.inverse_lat_hbm, ...), custom_call_target="tpu_custom_call" | custom-call | tf_op jit(solution)/shard_map/pallas_call | solution.py:802
  17.7 0.6 %copy.10 = f32[2,6,1440]{2,0,1:T(2,128)} copy(f32[2,6,1440]{2,0,1:T(2,128)S(1)} %bitcast.4) | data formatting | bytes 138240

commit v2 on v1

--- a/solution.py
+++ b/solution.py
@@ -231,20 +231,27 @@
     ]
     devices = [(time, band) for time in range(times) for band in range(bands)]
     chosen = sorted(devices, key=lambda d: (hops(*d, times, bands), d))[: len(jobs)]
-    owner, free = {}, []
-    for band in range(bands):
-        local = sorted(d for d in chosen if d[1] == band)
-        for kind, device in enumerate(local[:KINDS]):
-            owner[band, kind] = device
-        free.extend(local[KINDS:])
-    free.sort(key=lambda d: -hops(*d, times, bands))
-    sources, used = {}, {}
-    for job in jobs:
-        if job not in owner:
-            owner[job] = free.pop(0)
-            sources[job] = (used.get(job[0], 0), job[0])
-            used[job[0]] = sources[job][0] + 1
+    owner, sources, used = {}, {}, {}
+    for side in range(2):
+        pool = sorted(d for d in chosen if d[0] % 2 == side)
+        wanted = [job for job in jobs if job[0] // cosines == side]
+        for band in range(side * cosines, (side + 1) * cosines):
+            for kind, device in enumerate([d for d in pool if d[1] == band][:KINDS]):
+                owner[band, kind] = device
+        taken = set(owner.values())
+        free = sorted((d for d in pool if d not in taken), key=lambda d: -hops(*d, times, bands))
+        for job in wanted:
+            if job not in owner:
+                owner[job] = free.pop(0)
+                sources[job] = (used.get(job[0], 0), job[0])
+                used[job[0]] = sources[job][0] + 1
     return jobs, [owner[job] for job in jobs], [sources.get(job) for job in jobs]
+
+
+def balanced(times, bands):
+    every = sorted(hops(time, band, times, bands) for time in range(times) for band in range(bands))
+    wanted = KINDS * bands
+    return wanted < len(every) and every[wanted - 1] < every[wanted]
 
 
 def mode_columns(modes_dev):
@@ -285,7 +292,7 @@
     tables = tables.astype(np.float32)
     high = tables.astype(jnp.bfloat16)
     low = (tables - high.astype(np.float32)).astype(jnp.bfloat16)
-    return high, low
+    return np.stack([high, low], axis=1)
 
 
 def lat_tables(lat_size, bands):
@@ -390,17 +397,14 @@
     scale_hbm,
     forward_lat_hbm,
     inverse_lat_hbm,
-    high_hbm,
-    low_hbm,
+    table_hbm,
     out_ref,
     observed_ref,
     noise_ref,
-    variance_ref,
-    scale_ref,
+    block_ref,
     forward_lat_ref,
     inverse_lat_ref,
-    high,
-    low,
+    table,
     folded,
     outbox,
     inbox,
@@ -422,7 +426,6 @@
 ):
     devices = times * bands
     cosines = bands // 2
-    stride = 5 if devices % 5 else 1
     jobs, owners, sources = plan(times, bands)
     codes = [time * bands + band for time, band in owners]
     my_time = lax.axis_index("tm")
@@ -432,16 +435,10 @@
     half = lon_size // 2
     hours = gain_ref.shape[0]
     n_half = gain_ref.shape[2]
-    modes_dev = variance_ref.shape[1]
+    modes_dev = block_ref.shape[2]
     full, rest = mode_columns(modes_dev)
-    points = high.shape[2]
+    points = table.shape[3]
     mirror = half % LANES
-
-    def pick(index, values):
-        total = 0
-        for place, value in enumerate(values):
-            total = total + jnp.where(index == place, value, 0)
-        return total
 
     def mine(places, values):
         total = 0
@@ -449,24 +446,31 @@
             total = total + jnp.where(me == place, value, 0)
         return total
 
-    my_job = mine(codes, range(1, len(jobs) + 1)) - 1
-    owning = my_job >= 0
-    moved = [index for index, source in enumerate(sources) if source is not None]
-    source_codes = [sources[index][0] * bands + sources[index][1] for index in moved]
-    lending = mine(source_codes, [1] * len(moved)) > 0
-    borrowing = mine([codes[index] for index in moved], [1] * len(moved)) > 0
-
-    def table_copy(kind, which):
-        source, target = ((high_hbm, high), (low_hbm, low))[which]
-        return pltpu.make_async_copy(source.at[kind], target.at[kind], table_sem.at[kind, which])
+    deep = math.isqrt(bands // 2)
+    limit = max(hops(*owner, times, bands) for owner in owners)
+    row, core = my_time // 2, my_time % 2
+    plane, column = my_band // deep, my_band % deep
+
+    def flip(bit, turn):
+        return 1 - bit if turn else bit
+
+    rows = [flip(row, turn) for turn in range(2)]
+    near, peers = [], []
+    for turn in range(bands):
+        level = 2 * flip(plane // 2, turn // 4) + flip(plane % 2, turn // 2 % 2)
+        across = flip(column, turn % 2)
+        near.append(level + across)
+        peers.append(level * deep + across)
+    owning = row + near[0] <= limit
+
+    def table_copy(kind):
+        return pltpu.make_async_copy(table_hbm.at[kind], table.at[kind], table_sem.at[kind])
 
     inputs = [
         pltpu.make_async_copy(source, target, input_sem.at[index])
         for index, (source, target) in enumerate(
             [
                 (observed_hbm, observed_ref),
-                (variance_hbm, variance_ref),
-                (scale_hbm, scale_ref),
                 (noise_hbm, noise_ref),
                 (forward_lat_hbm, forward_lat_ref),
                 (inverse_lat_hbm, inverse_lat_ref),
@@ -474,6 +478,14 @@
         )
     ]
     inputs[0].start()
+    table_copy(0).start()
+    table_copy(1).start()
+    pltpu.make_async_copy(variance_hbm, block_ref.at[0], input_sem.at[4]).start()
+    pltpu.make_async_copy(scale_hbm, block_ref.at[1], input_sem.at[4]).start()
+    table_copy(2).start()
+    table_copy(3).start()
+    for copy in inputs[1:]:
+        copy.start()
     inbox[...] = jnp.zeros_like(inbox)
     inbox_back[...] = jnp.zeros_like(inbox_back)
 
@@ -481,20 +493,17 @@
 
     @pl.when(owning)
     def _():
-        def greet(step, carry):
-            peer = lax.rem(me + step, devices)
+        for turn in range(devices - 1, 0, -1):
+            time = 2 * rows[turn // bands // 2] + flip(core, turn // bands % 2)
             pl.semaphore_signal(
-                barrier, inc=1, device_id=(peer // bands, lax.rem(peer, bands)), device_id_type=MESH
+                barrier, inc=1, device_id=(time, peers[turn % bands]), device_id_type=MESH
             )
-            return carry
-
-        lax.fori_loop(1, devices, greet, 0)
-
-    for kind in range(4):
-        table_copy(kind, 0).start()
-        table_copy(kind, 1).start()
-    for copy in inputs[1:]:
-        copy.start()
+
+    my_job = mine(codes, range(1, len(jobs) + 1)) - 1
+    moved = [index for index, source in enumerate(sources) if source is not None]
+    source_codes = [sources[index][0] * bands + sources[index][1] for index in moved]
+    lending = mine(source_codes, [1] * len(moved)) > 0
+    borrowing = mine([codes[index] for index in moved], [1] * len(moved)) > 0
 
     def own_modes(ref, kind):
         mode = lax.broadcasted_iota(jnp.int32, (modes_dev, LANES), 0)
@@ -507,7 +516,7 @@
         picked = (mode == wanted).astype(jnp.float32)
         lane = lax.broadcasted_iota(jnp.int32, (n_half, LANES), 1)
         used = wanted[:n_half] < modes_dev
-        value = lax.dot_general(ref[...], picked, NN, precision=HIGHEST, preferred_element_type=jnp.float32)
+        value = lax.dot_general(ref, picked, NN, precision=HIGHEST, preferred_element_type=jnp.float32)
         value = jnp.where(lane < WIDTH, value[:n_half], value[n_half:])
         return jnp.where(used, value, 1.0)
 
@@ -547,12 +556,11 @@
     wide_lanes = cosines * WIDTH
 
     def forward(kind):
-        table_copy(kind, 0).wait()
-        table_copy(kind, 1).wait()
+        table_copy(kind).wait()
         upper, lower = split(jnp.concatenate(classes[kind], axis=0))
         both = jnp.concatenate([upper, lower], axis=0)
-        wide = lax.dot_general(both, high[kind], NT, preferred_element_type=jnp.float32)
-        fine = lax.dot_general(upper, low[kind], NT, preferred_element_type=jnp.float32)
+        wide = lax.dot_general(both, table[kind, 0], NT, preferred_element_type=jnp.float32)
+        fine = lax.dot_general(upper, table[kind, 1], NT, preferred_element_type=jnp.float32)
         return wide[: 2 * ROWS] + wide[2 * ROWS :] + fine
 
     def spin(value, amount):
@@ -561,7 +569,9 @@
 
     quarter = lane // QUARTER
     middle = None
-    for side in range(2):
+
+    def transform(side):
+        nonlocal middle
         found = [forward(2 * side), forward(2 * side + 1)]
         base = side * KINDS * cosines
         for parity in range(2):
@@ -570,10 +580,11 @@
                 first, second = swap_halves(block[:ROWS], block[ROWS:])
                 if side == 0 and parity == 0 and pair == 0:
                     middle = spin(first, 1)
+                    first = jnp.where(lax.rem(lane, WIDTH) == WIDTH - 1, 0.0, first)
                 if side == 1 and parity == 0 and pair == 0:
                     first = jnp.where(lax.rem(lane, WIDTH) == 0, pltpu.roll(middle, WIDTH, 1), first)
-                outbox[base + parity * cosines + 2 * pair] = first
-                outbox[base + parity * cosines + 2 * pair + 1] = second
+                outbox[codes[base + parity * cosines + 2 * pair]] = first
+                outbox[codes[base + parity * cosines + 2 * pair + 1]] = second
         mixed = [value[:, wide_lanes:] for value in found]
         for local in range(cosines):
             parts = [
@@ -582,27 +593,7 @@
             ]
             merged = jnp.where(quarter == 0, parts[0], parts[1])
             merged = jnp.where(quarter == 2, parts[2], merged)
-            outbox[base + 2 * cosines + local] = jnp.where(quarter == 3, parts[3], merged)
-
-    inputs[1].wait()
-    inputs[2].wait()
-
-    @pl.when(lending)
-    def _():
-        kind = mine(source_codes, [jobs[index][1] for index in moved])
-        params_out[0] = own_modes(variance_ref, kind)
-        params_out[1] = own_modes(scale_ref, kind)
-
-    @pl.when(owning)
-    def _():
-        kind = mine(codes, [kind for _, kind in jobs])
-
-        @pl.when(jnp.logical_not(borrowing))
-        def _():
-            params[0] = own_modes(variance_ref, kind)
-            params[1] = own_modes(scale_ref, kind)
-
-    pl.semaphore_wait(barrier, len(jobs) - owning.astype(jnp.int32))
+            outbox[codes[base + 2 * cosines + local]] = jnp.where(quarter == 3, parts[3], merged)
 
     def params_copy():
         target = mine(source_codes, [codes[index] for index in moved])
@@ -615,17 +606,13 @@
             device_id_type=MESH,
         )
 
-    @pl.when(lending)
-    def _():
-        params_copy().start()
-
     def exchange(box, landing, sends, recv, slot, peer, target):
         return pltpu.make_async_remote_copy(
             src_ref=box.at[slot, pl.ds(0, lat_dev)],
             dst_ref=landing.at[target, pl.ds(0, lat_dev)],
             send_sem=sends.at[0],
             recv_sem=recv,
-            device_id=(peer // bands, lax.rem(peer, bands)),
+            device_id=peer,
             device_id_type=MESH,
         )
 
@@ -638,24 +625,54 @@
         come = landing.at[pl.ds(first, count), pl.ds(0, lat_dev)]
         pltpu.make_async_copy(come, come, recv).wait()
 
-    for group in range(2 * KINDS):
-        for step in range(cosines):
-            local = lax.rem(me + step, cosines)
-            peer = pick(local, codes[group * cosines : (group + 1) * cosines])
-
-            @pl.when(peer != me)
-            def _():
-                exchange(outbox, inbox, send_sem, recv_sem.at[my_time], group * cosines + local, peer, me).start()
+    def send(side):
+        for turn in range(1, -1, -1):
+            time = 2 * rows[turn] + side
+            for other in range(bands - 1, -1, -1):
+                wanted = rows[turn] + near[other] <= limit
+                if turn == 0 and other == 0:
+                    wanted = wanted & (core != side)
+
+                @pl.when(wanted)
+                def _():
+                    exchange(
+                        outbox,
+                        inbox,
+                        send_sem,
+                        recv_sem.at[my_time],
+                        time * bands + peers[other],
+                        (time, peers[other]),
+                        me,
+                    ).start()
+
+    transform(0)
+    pl.semaphore_wait(barrier, len(jobs) - owning.astype(jnp.int32))
+    send(0)
+    pltpu.make_async_copy(block_ref, block_ref, input_sem.at[4]).wait()
+
+    @pl.when(lending)
+    def _():
+        kind = mine(source_codes, [jobs[index][1] for index in moved])
+        params_out[0] = own_modes(block_ref[0], kind)
+        params_out[1] = own_modes(block_ref[1], kind)
+        params_copy().start()
+
+    transform(1)
+    send(1)
+
+    for copy in inputs[1:]:
+        copy.wait()
 
     @pl.when(owning)
     def _():
-        keep(outbox, inbox, recv_sem.at[my_time], my_job, me).start()
-
-    for copy in inputs[3:]:
-        copy.wait()
-
-    @pl.when(owning)
-    def _():
+        keep(outbox, inbox, recv_sem.at[my_time], me, me).start()
+
+        @pl.when(jnp.logical_not(borrowing))
+        def _():
+            kind = mine(codes, [kind for _, kind in jobs])
+            params[0] = own_modes(block_ref[0], kind)
+            params[1] = own_modes(block_ref[1], kind)
+
         @pl.when(borrowing)
         def _():
             pltpu.make_async_copy(params, params, params_recv_sem.at[0]).wait()
@@ -695,55 +712,59 @@
             stacked = jnp.concatenate(swap_halves(series[2 * time], series[2 * time + 1]), axis=0)
             grid = paired_dot(inverse_lat_ref[...], stacked)
             outbox_back[time * bands : (time + 1) * bands] = grid.reshape(bands, ROWS, LANES)
-
-        def send_back(step, carry):
-            peer = lax.rem(me + step * stride, devices)
-            exchange(
-                outbox_back, inbox_back, send_back_sem, recv_back_sem.at[my_job // cosines], peer, peer, my_job
-            ).start()
-            return carry
-
-        lax.fori_loop(1, devices, send_back, 0)
-        keep(outbox_back, inbox_back, recv_back_sem.at[my_job // cosines], me, my_job).start()
-
-    sums = []
-    later = None
+            for other in range(bands - 1, -1, -1):
+                copy = exchange(
+                    outbox_back,
+                    inbox_back,
+                    send_back_sem,
+                    recv_back_sem.at[core],
+                    time * bands + peers[other],
+                    (time, peers[other]),
+                    my_job,
+                )
+                if other == 0:
+                    pl.when(my_time != time)(copy.start)
+                else:
+                    copy.start()
+
+        keep(outbox_back, inbox_back, recv_back_sem.at[core], me, my_job).start()
+
+    grids = []
     for side in range(2):
         base = side * KINDS * cosines
-        boxes = {}
-        for group in ((2, 0, 1) if side == 0 else (0, 2, 1)):
-            landed(inbox_back, recv_back_sem.at[side * KINDS + group], base + group * cosines, cosines)
-            for local in range(cosines):
-                boxes[group, local] = inbox_back[base + group * cosines + local]
-        shared = [[], []]
-        for hour in range(2):
-            for parity in range(2):
-                merged = None
-                for local in range(cosines):
-                    moved_part = spin(boxes[2, local], (local - (2 * hour + parity)) * QUARTER)
-                    merged = moved_part if merged is None else jnp.where(quarter == local, moved_part, merged)
-                shared[parity].append(merged)
+        landed(inbox_back, recv_back_sem.at[side], base, KINDS * cosines)
+        boxes = [
+            [inbox_back[base + kind * cosines + local] for local in range(cosines)] for kind in range(KINDS)
+        ]
         for parity in range(2):
             blocks = []
             for pair in range(cosines // 2):
-                first, second = swap_halves(boxes[parity, 2 * pair], boxes[parity, 2 * pair + 1])
-                blocks.append([first, second])
-            blocks.append(shared[parity])
-            sums.append(blocks)
+                blocks.append(list(swap_halves(*boxes[parity][2 * pair : 2 * pair + 2])))
+            shared = []
+            for hour in range(2):
+                merged = None
+                for local in range(cosines):
+                    part = spin(boxes[2][local], (local - (2 * hour + parity)) * QUARTER)
+                    merged = part if merged is None else jnp.where(quarter == local, part, merged)
+                shared.append(merged)
+            blocks.append(shared)
+            upper, lower = split(
+                jnp.concatenate([jnp.concatenate(block, axis=0) for block in blocks], axis=1)
+            )
+            both = jnp.concatenate([upper, lower], axis=0)
+            kind = 2 * side + parity
+            wide = lax.dot_general(both, table[kind, 0], NN, preferred_element_type=jnp.float32)
+            fine = lax.dot_general(upper, table[kind, 1], NN, preferred_element_type=jnp.float32)
+            grids.append(wide[: 2 * ROWS] + wide[2 * ROWS :] + fine)
+
     origin = inbox_back[KINDS * cosines]
+    alternating = jnp.where(lax.rem(lane, 2) == 0, 1.0, -1.0) * math.sqrt(1.0 / lon_size)
+    lifted = []
     for hour in range(2):
-        shift = WIDTH - 1 - hour * WIDTH
-        sums[0][0][hour] = jnp.where(lane == WIDTH - 1, spin(origin, shift), sums[0][0][hour])
-
-    grids = []
-    for kind in range(4):
-        upper, lower = split(
-            jnp.concatenate([jnp.concatenate(block, axis=0) for block in sums[kind]], axis=1)
-        )
-        both = jnp.concatenate([upper, lower], axis=0)
-        wide = lax.dot_general(both, high[kind], NN, preferred_element_type=jnp.float32)
-        fine = lax.dot_general(upper, low[kind], NN, preferred_element_type=jnp.float32)
-        grids.append(wide[: 2 * ROWS] + wide[2 * ROWS :] + fine)
+        value = jnp.broadcast_to(origin[:, hour * WIDTH : hour * WIDTH + 1], (ROWS, LANES)) * alternating
+        edge = jnp.where(lane == half // 2 % LANES, 0.5 * value, value)
+        lifted.append(jnp.concatenate([value] * (points // LANES - 1) + [edge], axis=1))
+    grids[0] = grids[0] + jnp.concatenate(lifted, axis=0)
 
     count = points // LANES
     for hour in range(2):
@@ -792,7 +813,7 @@
     half_padded = round_up(lon_size // 2, LANES)
     n_jobs = KINDS * bands
 
-    high, low = lon_tables(lon_size, bands)
+    table = lon_tables(lon_size, bands)
     forward_lat, inverse_lat = lat_tables(lat_size, bands)
     in_vmem = pl.BlockSpec(memory_space=pltpu.VMEM)
     in_place = pl.BlockSpec(memory_space=pltpu.HBM)
@@ -802,19 +823,17 @@
     field = pl.pallas_call(
         functools.partial(smoother_kernel, times, bands),
         out_shape=pltpu.VMEM((lat_dev, hours_dev, lon_size), jnp.float32),
-        in_specs=[in_place] * 8,
+        in_specs=[in_place] * 7,
         out_specs=in_vmem,
         scratch_shapes=[
             pltpu.VMEM((lat_dev, hours_dev, lon_size), jnp.float32),
             pltpu.SMEM((hours,), jnp.float32),
-            pltpu.VMEM((lat_size, spectral_var.shape[0]), jnp.float32),
-            pltpu.VMEM((lat_size, spectral_var.shape[0]), jnp.float32),
+            pltpu.VMEM((2, lat_size, spectral_var.shape[0]), jnp.float32),
             pltpu.VMEM(forward_lat.shape, jnp.bfloat16),
             pltpu.VMEM(inverse_lat.shape, jnp.bfloat16),
-            pltpu.VMEM(high.shape, jnp.bfloat16),
-            pltpu.VMEM(low.shape, jnp.bfloat16),
+            pltpu.VMEM(table.shape, jnp.bfloat16),
             pltpu.VMEM((2, 2, ROWS, half_padded), jnp.float32),
-            job_box,
+            box,
             box,
             box,
             job_box,
@@ -823,12 +842,12 @@
             pltpu.VMEM((3, 3, n_half, LANES), jnp.float32),
             pltpu.VMEM((hours, 3, n_half, LANES), jnp.float32),
             pltpu.VMEM((hours, 3, 3, n_half, LANES), jnp.float32),
-            dma((6,)),
-            dma((4, 2)),
+            dma((5,)),
+            dma((4,)),
             dma((1,)),
             dma((times,)),
             dma((1,)),
-            dma((2 * KINDS,)),
+            dma((2,)),
             dma((1,)),
             dma((1,)),
         ],
@@ -840,8 +859,7 @@
         time_scale.T,
         jnp.asarray(forward_lat),
         jnp.asarray(inverse_lat),
-        jnp.asarray(high),
-        jnp.asarray(low),
+        jnp.asarray(table),
     )
     return field.transpose(1, 0, 2)
 
@@ -857,6 +875,7 @@
         and lat_dev <= ROWS
         and lat_size % (2 * ROWS) == 0
         and times == KINDS + 1
+        and balanced(times, bands)
         and 2 * math.isqrt(bands // 2) ** 2 == bands
         and bands == LANES // 16
         and lon_size % 4 == 0

time: 18.5 us -> 17.6 us (0.951)
  Pallas kernels: 17.7 us -> 16.8 us
    pallas_call x1, Pallas kernels: 17.7 us -> 16.8 us  [per_device_fused(): pl.pallas_call(functools.partial(smoother_kernel, times, bands), out_shap...]
where the time goes in v2:
time: 17.6 us; the launch traced here: 17.5 us
  Pallas kernels  16.8 us (95%)
  local copies, waits for them, and re-layouts  0.64 us (4%)
    pallas_call x1, Pallas kernels, per_device_fused(): pl.pallas_call(functools.partial(smoother_kernel, times, bands), out_shap...  16.8 us
    unnamed x1, local copies, waits for them, and re-layouts  0.64 us

profile of v2, /device:TPU:0, one launch (start us, length us, event | category | flops | bytes accessed | tf_op | source)
XLA Modules:
  0.0 17.5 jit_solution(15626601762805073043)
XLA Ops:
  0.0 16.8 %shard_map.73 = f32[6,2,1440]{2,1,0:T(2,128)S(1)} custom-call(f32[6,2,1440]{2,1,0:T(2,128)} %bitcast.5, f32[8]{0:T(128)} %noise_hbm.1, f32[48,180]{1,0:T(8,128)} %bitcast.6, f32[48,180]{1,0:T(8,128)} %bitcast.7, bf16[96,64]{1,0:T(8,128)(2,1)} %constant.6.clone.forward_lat_hbm, bf16[128,48]{1,0:T(8,128)(2,1)} %constant.7.clone.inverse_lat_hbm, ...), custom_call_target="tpu_custom_call" | custom-call | tf_op jit(solution)/shard_map/pallas_call | solution.py:823
  16.8 0.6 %copy.9 = f32[2,6,1440]{2,0,1:T(2,128)} copy(f32[2,6,1440]{2,0,1:T(2,128)S(1)} %bitcast.4) | data formatting | bytes 138240

commit v3 on v2

--- a/solution.py
+++ b/solution.py
@@ -232,26 +232,24 @@
     devices = [(time, band) for time in range(times) for band in range(bands)]
     chosen = sorted(devices, key=lambda d: (hops(*d, times, bands), d))[: len(jobs)]
     owner, sources, used = {}, {}, {}
-    for side in range(2):
-        pool = sorted(d for d in chosen if d[0] % 2 == side)
-        wanted = [job for job in jobs if job[0] // cosines == side]
-        for band in range(side * cosines, (side + 1) * cosines):
-            for kind, device in enumerate([d for d in pool if d[1] == band][:KINDS]):
-                owner[band, kind] = device
-        taken = set(owner.values())
-        free = sorted((d for d in pool if d not in taken), key=lambda d: -hops(*d, times, bands))
-        for job in wanted:
-            if job not in owner:
-                owner[job] = free.pop(0)
-                sources[job] = (used.get(job[0], 0), job[0])
-                used[job[0]] = sources[job][0] + 1
+    for band in range(bands):
+        for kind, device in enumerate(sorted(d for d in chosen if d[1] == band)[:KINDS]):
+            owner[band, kind] = device
+    taken = set(owner.values())
+    free = sorted((d for d in chosen if d not in taken), key=lambda d: -hops(*d, times, bands))
+    for job in jobs:
+        if job not in owner:
+            owner[job] = free.pop(0)
+            sources[job] = (used.get(job[0], 0), job[0])
+            used[job[0]] = sources[job][0] + 1
     return jobs, [owner[job] for job in jobs], [sources.get(job) for job in jobs]
 
 
 def balanced(times, bands):
     every = sorted(hops(time, band, times, bands) for time in range(times) for band in range(bands))
     wanted = KINDS * bands
-    return wanted < len(every) and every[wanted - 1] < every[wanted]
+    lower = max(hops(time, band, times, bands) for time in range(times) for band in range(bands // 2))
+    return wanted < len(every) and lower <= every[wanted - 1] < every[wanted]
 
 
 def mode_columns(modes_dev):
@@ -406,9 +404,13 @@
     inverse_lat_ref,
     table,
     folded,
-    outbox,
+    outbox_cos,
+    outbox_sin,
     inbox,
-    outbox_back,
+    back_0,
+    back_1,
+    back_2,
+    back_3,
     inbox_back,
     params_out,
     params,
@@ -426,6 +428,8 @@
 ):
     devices = times * bands
     cosines = bands // 2
+    outboxes = (outbox_cos, outbox_sin)
+    boxes_back = (back_0, back_1, back_2, back_3)
     jobs, owners, sources = plan(times, bands)
     codes = [time * bands + band for time, band in owners]
     my_time = lax.axis_index("tm")
@@ -477,11 +481,11 @@
             ]
         )
     ]
+    pltpu.make_async_copy(variance_hbm, block_ref.at[0], input_sem.at[4]).start()
+    pltpu.make_async_copy(scale_hbm, block_ref.at[1], input_sem.at[4]).start()
     inputs[0].start()
     table_copy(0).start()
     table_copy(1).start()
-    pltpu.make_async_copy(variance_hbm, block_ref.at[0], input_sem.at[4]).start()
-    pltpu.make_async_copy(scale_hbm, block_ref.at[1], input_sem.at[4]).start()
     table_copy(2).start()
     table_copy(3).start()
     for copy in inputs[1:]:
@@ -521,6 +525,14 @@
         return jnp.where(used, value, 1.0)
 
     folded[...] = jnp.zeros_like(folded)
+    pltpu.make_async_copy(block_ref, block_ref, input_sem.at[4]).wait()
+
+    @pl.when(lending)
+    def _():
+        kind = mine(source_codes, [jobs[index][1] for index in moved])
+        params_out[0] = own_modes(block_ref[0], kind)
+        params_out[1] = own_modes(block_ref[1], kind)
+
     inputs[0].wait()
     lane = lax.broadcasted_iota(jnp.int32, (ROWS, LANES), 1)
     reverse = lax.rem(mirror + LANES - lane, LANES)
@@ -583,8 +595,8 @@
                     first = jnp.where(lax.rem(lane, WIDTH) == WIDTH - 1, 0.0, first)
                 if side == 1 and parity == 0 and pair == 0:
                     first = jnp.where(lax.rem(lane, WIDTH) == 0, pltpu.roll(middle, WIDTH, 1), first)
-                outbox[codes[base + parity * cosines + 2 * pair]] = first
-                outbox[codes[base + parity * cosines + 2 * pair + 1]] = second
+                outboxes[side][codes[base + parity * cosines + 2 * pair]] = first
+                outboxes[side][codes[base + parity * cosines + 2 * pair + 1]] = second
         mixed = [value[:, wide_lanes:] for value in found]
         for local in range(cosines):
             parts = [
@@ -593,7 +605,7 @@
             ]
             merged = jnp.where(quarter == 0, parts[0], parts[1])
             merged = jnp.where(quarter == 2, parts[2], merged)
-            outbox[codes[base + 2 * cosines + local]] = jnp.where(quarter == 3, parts[3], merged)
+            outboxes[side][codes[base + 2 * cosines + local]] = jnp.where(quarter == 3, parts[3], merged)
 
     def params_copy():
         target = mine(source_codes, [codes[index] for index in moved])
@@ -625,38 +637,46 @@
         come = landing.at[pl.ds(first, count), pl.ds(0, lat_dev)]
         pltpu.make_async_copy(come, come, recv).wait()
 
+    def forth(box, time, band, wanted):
+        @pl.when(wanted)
+        def _():
+            exchange(
+                box, inbox, send_sem, recv_sem.at[my_time], time * bands + band, (time, band), me
+            ).start()
+
+    upper_half = plane // 2
+
+    def place(top, turn):
+        level = 2 * top + flip(plane % 2, turn // 2)
+        across = flip(column, turn % 2)
+        return level * deep + across, level + across
+
     def send(side):
-        for turn in range(1, -1, -1):
-            time = 2 * rows[turn] + side
-            for other in range(bands - 1, -1, -1):
-                wanted = rows[turn] + near[other] <= limit
+        for turn in range(times - 1, -1, -1):
+            next_row, next_core = rows[turn // 2], flip(core, turn % 2)
+            for other in range(deep * deep - 1, -1, -1):
+                band, height = place(side, other)
+                if side == 0:
+                    wanted = next_row + next_core < 2
+                else:
+                    wanted = next_row + height <= limit
                 if turn == 0 and other == 0:
-                    wanted = wanted & (core != side)
-
-                @pl.when(wanted)
-                def _():
-                    exchange(
-                        outbox,
-                        inbox,
-                        send_sem,
-                        recv_sem.at[my_time],
-                        time * bands + peers[other],
-                        (time, peers[other]),
-                        me,
-                    ).start()
+                    wanted = wanted & (upper_half != side)
+                forth(outboxes[side], 2 * next_row + next_core, band, wanted)
+        if side == 1:
+            for other in range(deep * deep - 1, -1, -1):
+                band, _ = place(0, other)
+                wanted = (my_time != times - 1) | (upper_half != 0) if other == 0 else my_time >= 0
+                forth(outboxes[1], times - 1, band, wanted)
 
     transform(0)
     pl.semaphore_wait(barrier, len(jobs) - owning.astype(jnp.int32))
-    send(0)
-    pltpu.make_async_copy(block_ref, block_ref, input_sem.at[4]).wait()
 
     @pl.when(lending)
     def _():
-        kind = mine(source_codes, [jobs[index][1] for index in moved])
-        params_out[0] = own_modes(block_ref[0], kind)
-        params_out[1] = own_modes(block_ref[1], kind)
         params_copy().start()
 
+    send(0)
     transform(1)
     send(1)
 
@@ -665,7 +685,9 @@
 
     @pl.when(owning)
     def _():
-        keep(outbox, inbox, recv_sem.at[my_time], me, me).start()
+        for side in range(2):
+            inside = (my_job < KINDS * cosines) == (side == 0)
+            pl.when(inside)(keep(outboxes[side], inbox, recv_sem.at[my_time], me, me).start)
 
         @pl.when(jnp.logical_not(borrowing))
         def _():
@@ -679,21 +701,22 @@
 
         symmetric_gains(noise_ref, params[0], params[1], transition_ref, gain_ref, smoother_ref)
 
-        spectra = []
+        transition = [[transition_ref[row, column] for column in range(3)] for row in range(3)]
+        means, predictions = [], []
         for time in range(times):
             landed(inbox, recv_sem.at[time], time * bands, bands)
             arrived = inbox[time * bands : (time + 1) * bands].reshape(bands * ROWS, LANES)
             mixed = paired_dot(forward_lat_ref[...], arrived)
-            spectra.extend(swap_halves(mixed[:n_half], mixed[n_half:]))
-
-        transition = [[transition_ref[row, column] for column in range(3)] for row in range(3)]
-        means, predictions = [], [None]
-        means.append([gain_ref[0, row] * spectra[0] for row in range(3)])
-        for hour in range(1, hours):
-            predicted = mat_vec(transition, means[-1])
-            residual = spectra[hour] - predicted[0]
-            predictions.append(predicted)
-            means.append([predicted[row] + gain_ref[hour, row] * residual for row in range(3)])
+            for hour, spectrum in enumerate(swap_halves(mixed[:n_half], mixed[n_half:]), 2 * time):
+                if hour == 0:
+                    predictions.append(None)
+                    means.append([gain_ref[0, row] * spectrum for row in range(3)])
+                    continue
+                predicted = mat_vec(transition, means[-1])
+                residual = spectrum - predicted[0]
+                predictions.append(predicted)
+                means.append([predicted[row] + gain_ref[hour, row] * residual for row in range(3)])
+        recv_back = recv_back_sem.at[my_job // (KINDS * cosines)]
         smoothed = means[-1]
         series = [None] * hours
         series[hours - 1] = smoothed[0]
@@ -711,14 +734,14 @@
         for time in range(times):
             stacked = jnp.concatenate(swap_halves(series[2 * time], series[2 * time + 1]), axis=0)
             grid = paired_dot(inverse_lat_ref[...], stacked)
-            outbox_back[time * bands : (time + 1) * bands] = grid.reshape(bands, ROWS, LANES)
+            boxes_back[time][...] = grid.reshape(bands, ROWS, LANES)
             for other in range(bands - 1, -1, -1):
                 copy = exchange(
-                    outbox_back,
+                    boxes_back[time],
                     inbox_back,
                     send_back_sem,
-                    recv_back_sem.at[core],
-                    time * bands + peers[other],
+                    recv_back,
+                    peers[other],
                     (time, peers[other]),
                     my_job,
                 )
@@ -727,7 +750,8 @@
                 else:
                     copy.start()
 
-        keep(outbox_back, inbox_back, recv_back_sem.at[core], me, my_job).start()
+        for time in range(times):
+            pl.when(my_time == time)(keep(boxes_back[time], inbox_back, recv_back, my_band, my_job).start)
 
     grids = []
     for side in range(2):
@@ -790,15 +814,15 @@
         left = box.at[pl.ds(0, count), pl.ds(0, lat_dev)]
         pltpu.make_async_copy(left, left, sends.at[0]).wait()
 
-    gone(outbox, send_sem, len(jobs) - 1)
+    gone(inbox, send_sem, len(jobs) - 1)
 
     @pl.when(jnp.logical_not(owning))
     def _():
-        gone(outbox, send_sem, 1)
+        gone(inbox, send_sem, 1)
 
     @pl.when(owning)
     def _():
-        gone(outbox_back, send_back_sem, devices - 1)
+        gone(inbox, send_back_sem, devices - 1)
 
     @pl.when(lending)
     def _():
@@ -818,6 +842,7 @@
     in_vmem = pl.BlockSpec(memory_space=pltpu.VMEM)
     in_place = pl.BlockSpec(memory_space=pltpu.HBM)
     box = pltpu.VMEM((times * bands, ROWS, LANES), jnp.float32)
+    band_box = pltpu.VMEM((bands, ROWS, LANES), jnp.float32)
     job_box = pltpu.VMEM((n_jobs, ROWS, LANES), jnp.float32)
     dma = pltpu.SemaphoreType.DMA
     field = pl.pallas_call(
@@ -836,6 +861,10 @@
             box,
             box,
             box,
+            band_box,
+            band_box,
+            band_box,
+            band_box,
             job_box,
             pltpu.VMEM((2, n_half, LANES), jnp.float32),
             pltpu.VMEM((2, n_half, LANES), jnp.float32),

time: 17.6 us -> 17 us (0.966)
  Pallas kernels: 16.8 us -> 16.2 us
    pallas_call x1, Pallas kernels: 16.8 us -> 16.2 us  [per_device_fused(): pl.pallas_call(functools.partial(smoother_kernel, times, bands), out_shap...]
where the time goes in v3:
time: 17 us; the launch traced here: 16.9 us
  Pallas kernels  16.2 us (95%)
  local copies, waits for them, and re-layouts  0.64 us (4%)
    pallas_call x1, Pallas kernels, per_device_fused(): pl.pallas_call(functools.partial(smoother_kernel, times, bands), out_shap...  16.2 us
    unnamed x1, local copies, waits for them, and re-layouts  0.64 us

profile of v3, /device:TPU:0, one launch (start us, length us, event | category | flops | bytes accessed | tf_op | source)
XLA Modules:
  0.0 16.9 jit_solution(4108281476904385092)
XLA Ops:
  0.0 16.2 %shard_map.73 = f32[6,2,1440]{2,1,0:T(2,128)S(1)} custom-call(f32[6,2,1440]{2,1,0:T(2,128)} %bitcast.5, f32[8]{0:T(128)} %noise_hbm.1, f32[48,180]{1,0:T(8,128)} %bitcast.6, f32[48,180]{1,0:T(8,128)} %bitcast.7, bf16[96,64]{1,0:T(8,128)(2,1)} %constant.6.clone.forward_lat_hbm, bf16[128,48]{1,0:T(8,128)(2,1)} %constant.7.clone.inverse_lat_hbm, ...), custom_call_target="tpu_custom_call" | custom-call | tf_op jit(solution)/shard_map/pallas_call | solution.py:848
  16.3 0.6 %copy.9 = f32[2,6,1440]{2,0,1:T(2,128)} copy(f32[2,6,1440]{2,0,1:T(2,128)S(1)} %bitcast.4) | data formatting | bytes 138240

commit v4 on v3

--- a/solution.py
+++ b/solution.py
@@ -221,6 +221,11 @@
     return time // 2 + band // wide + band % wide
 
 
+def spare(time, band, bands):
+    level = band // math.isqrt(bands // 2)
+    return time % 2 == 1 and time // 2 + level == 1
+
+
 def plan(times, bands):
     cosines = bands // 2
     jobs = [
@@ -233,7 +238,8 @@
     chosen = sorted(devices, key=lambda d: (hops(*d, times, bands), d))[: len(jobs)]
     owner, sources, used = {}, {}, {}
     for band in range(bands):
-        for kind, device in enumerate(sorted(d for d in chosen if d[1] == band)[:KINDS]):
+        local = sorted((d for d in chosen if d[1] == band), key=lambda d: (spare(*d, bands), d))
+        for kind, device in enumerate(local[:KINDS]):
             owner[band, kind] = device
     taken = set(owner.values())
     free = sorted((d for d in chosen if d not in taken), key=lambda d: -hops(*d, times, bands))
@@ -509,7 +515,7 @@
     lending = mine(source_codes, [1] * len(moved)) > 0
     borrowing = mine([codes[index] for index in moved], [1] * len(moved)) > 0
 
-    def own_modes(ref, kind):
+    def own_modes(kind, target):
         mode = lax.broadcasted_iota(jnp.int32, (modes_dev, LANES), 0)
         slot = lax.rem(lax.broadcasted_iota(jnp.int32, (modes_dev, LANES), 1), WIDTH)
         second = (slot >= QUARTER).astype(jnp.int32)
@@ -517,21 +523,26 @@
         whole = jnp.where(slot < full, 2 * slot + kind, modes_dev)
         mixed = jnp.where(place < rest, 2 * (full + place) + second, modes_dev)
         wanted = jnp.where(kind == KINDS - 1, mixed, whole)
-        picked = (mode == wanted).astype(jnp.float32)
+        picked = (mode == wanted).astype(jnp.float32).astype(jnp.bfloat16)
         lane = lax.broadcasted_iota(jnp.int32, (n_half, LANES), 1)
         used = wanted[:n_half] < modes_dev
-        value = lax.dot_general(ref, picked, NN, precision=HIGHEST, preferred_element_type=jnp.float32)
-        value = jnp.where(lane < WIDTH, value[:n_half], value[n_half:])
-        return jnp.where(used, value, 1.0)
+        block = block_ref[...].reshape(4 * n_half, modes_dev)
+        high = block.astype(jnp.bfloat16)
+        left = block - high.astype(jnp.float32)
+        parts = jnp.concatenate([high, *split(left)], axis=0)
+        value = lax.dot_general(parts, picked, NN, preferred_element_type=jnp.float32)
+        value = value[: 4 * n_half] + value[4 * n_half : 8 * n_half] + value[8 * n_half :]
+        for index in range(2):
+            lower = value[2 * index * n_half : (2 * index + 1) * n_half]
+            upper = value[(2 * index + 1) * n_half : (2 * index + 2) * n_half]
+            target[index] = jnp.where(used, jnp.where(lane < WIDTH, lower, upper), 1.0)
 
     folded[...] = jnp.zeros_like(folded)
     pltpu.make_async_copy(block_ref, block_ref, input_sem.at[4]).wait()
 
     @pl.when(lending)
     def _():
-        kind = mine(source_codes, [jobs[index][1] for index in moved])
-        params_out[0] = own_modes(block_ref[0], kind)
-        params_out[1] = own_modes(block_ref[1], kind)
+        own_modes(mine(source_codes, [jobs[index][1] for index in moved]), params_out)
 
     inputs[0].wait()
     lane = lax.broadcasted_iota(jnp.int32, (ROWS, LANES), 1)
@@ -657,7 +668,7 @@
             for other in range(deep * deep - 1, -1, -1):
                 band, height = place(side, other)
                 if side == 0:
-                    wanted = next_row + next_core < 2
+                    wanted = (next_core == 0) | (next_row + flip(plane % 2, other // 2) != 1)
                 else:
                     wanted = next_row + height <= limit
                 if turn == 0 and other == 0:
@@ -666,8 +677,9 @@
         if side == 1:
             for other in range(deep * deep - 1, -1, -1):
                 band, _ = place(0, other)
-                wanted = (my_time != times - 1) | (upper_half != 0) if other == 0 else my_time >= 0
-                forth(outboxes[1], times - 1, band, wanted)
+                time = 2 * (1 - flip(plane % 2, other // 2)) + 1
+                wanted = (my_time != time) | (upper_half != 0) if other == 0 else my_time >= 0
+                forth(outboxes[1], time, band, wanted)
 
     transform(0)
     pl.semaphore_wait(barrier, len(jobs) - owning.astype(jnp.int32))
@@ -691,9 +703,7 @@
 
         @pl.when(jnp.logical_not(borrowing))
         def _():
-            kind = mine(codes, [kind for _, kind in jobs])
-            params[0] = own_modes(block_ref[0], kind)
-            params[1] = own_modes(block_ref[1], kind)
+            own_modes(mine(codes, [kind for _, kind in jobs]), params)
 
         @pl.when(borrowing)
         def _():
@@ -703,11 +713,15 @@
 
         transition = [[transition_ref[row, column] for column in range(3)] for row in range(3)]
         means, predictions = [], []
-        for time in range(times):
-            landed(inbox, recv_sem.at[time], time * bands, bands)
-            arrived = inbox[time * bands : (time + 1) * bands].reshape(bands * ROWS, LANES)
-            mixed = paired_dot(forward_lat_ref[...], arrived)
-            for hour, spectrum in enumerate(swap_halves(mixed[:n_half], mixed[n_half:]), 2 * time):
+        for first in range(0, times, 2):
+            spectra = []
+            for time in (first, first + 1):
+                landed(inbox, recv_sem.at[time], time * bands, bands)
+            for time in (first, first + 1):
+                arrived = inbox[time * bands : (time + 1) * bands].reshape(bands * ROWS, LANES)
+                mixed = paired_dot(forward_lat_ref[...], arrived)
+                spectra.extend(swap_halves(mixed[:n_half], mixed[n_half:]))
+            for hour, spectrum in enumerate(spectra, 2 * first):
                 if hour == 0:
                     predictions.append(None)
                     means.append([gain_ref[0, row] * spectrum for row in range(3)])

time: 17 us -> 16.8 us (0.988)
  Pallas kernels: 16.2 us -> 16 us
    pallas_call x1, Pallas kernels: 16.2 us -> 16 us  [per_device_fused(): pl.pallas_call(functools.partial(smoother_kernel, times, bands), out_shap...]
where the time goes in v4:
time: 16.8 us; the launch traced here: 16.7 us
  Pallas kernels  16 us (95%)
  local copies, waits for them, and re-layouts  0.64 us (4%)
    pallas_call x1, Pallas kernels, per_device_fused(): pl.pallas_call(functools.partial(smoother_kernel, times, bands), out_shap...  16 us
    unnamed x1, local copies, waits for them, and re-layouts  0.64 us

profile of v4, /device:TPU:0, one launch (start us, length us, event | category | flops | bytes accessed | tf_op | source)
XLA Modules:
  0.0 16.7 jit_solution(9328136235235416365)
XLA Ops:
  0.0 16.0 %shard_map.73 = f32[6,2,1440]{2,1,0:T(2,128)S(1)} custom-call(f32[6,2,1440]{2,1,0:T(2,128)} %bitcast.5, f32[8]{0:T(128)} %noise_hbm.1, f32[48,180]{1,0:T(8,128)} %bitcast.6, f32[48,180]{1,0:T(8,128)} %bitcast.7, bf16[96,64]{1,0:T(8,128)(2,1)} %constant.6.clone.forward_lat_hbm, bf16[128,48]{1,0:T(8,128)(2,1)} %constant.7.clone.inverse_lat_hbm, ...), custom_call_target="tpu_custom_call" | custom-call | tf_op jit(solution)/shard_map/pallas_call | solution.py:862
  16.0 0.6 %copy.9 = f32[2,6,1440]{2,0,1:T(2,128)} copy(f32[2,6,1440]{2,0,1:T(2,128)S(1)} %bitcast.4) | data formatting | bytes 138240
